TPU v7x, 32 devices: a whole 2x2x4 slice. The times are simulated.
32 devices in a mesh: fsdp: 4 (over x, core), ctx: 2 (over y), tp: 4 (over z).
Axes of the slice: x: 2, y: 2, z: 4, core: 2. Of those that a mesh axis runs over, the one named last changes fastest.
Arguments:
- layer_in: bfloat16 [16, 512, 1024], P('fsdp', ('ctx', 'tp')), may hold values from -6 to 6
- lengths: int32 [16], P('fsdp'), may hold values from 128 to 512, as said below
- cotangent: bfloat16 [16, 512, 1024], P('fsdp', ('ctx', 'tp')), may hold values from -6 to 6
- w_query: bfloat16 [1024, 1024], P('fsdp', 'tp'), may hold values from -0.1875 to 0.1875
- w_key: bfloat16 [1024, 1024], P('fsdp', 'tp'), may hold values from -0.1875 to 0.1875
- w_value: bfloat16 [1024, 1024], P('fsdp', 'tp'), may hold values from -0.1875 to 0.1875
- b_query: bfloat16 [1024], P(('tp', 'fsdp')), may hold values from -0.59765625 to 0.59765625
- b_value: bfloat16 [1024], P(('tp', 'fsdp')), may hold values from -0.29882812 to 0.29882812
- w_out: bfloat16 [1024, 1024], P('tp', 'fsdp'), may hold values from -2 to 2
- b_out: bfloat16 [1024], P('fsdp'), may hold values from -0.59765625 to 0.59765625
- gain_attn: bfloat16 [1024], P('fsdp'), may hold values from 0.099609375 to 1.8984375
- shift_attn: bfloat16 [1024], P('fsdp'), may hold values from -0.59765625 to 0.59765625
- w_up: bfloat16 [1024, 4096], P('fsdp', 'tp'), may hold values from -0.1875 to 0.1875
- b_up: bfloat16 [4096], P(('tp', 'fsdp')), may hold values from -0.59765625 to 0.59765625
- w_down: bfloat16 [4096, 1024], P('tp', 'fsdp'), may hold values from -0.09375 to 0.09375
- b_down: bfloat16 [1024], P('fsdp'), may hold values from -0.59765625 to 0.59765625
- gain_ffn: bfloat16 [1024], P('fsdp'), may hold values from 0.099609375 to 1.8984375
- shift_ffn: bfloat16 [1024], P('fsdp'), may hold values from -0.59765625 to 0.59765625
Outputs:
- layer_out: bfloat16 [16, 512, 1024], P('fsdp', ('ctx', 'tp'))
- input_grad: bfloat16 [16, 512, 1024], P('fsdp', ('ctx', 'tp'))
- grad_w_query: float32 [1024, 1024], P('fsdp', 'tp')
- grad_w_key: float32 [1024, 1024], P('fsdp', 'tp')
- grad_w_value: float32 [1024, 1024], P('fsdp', 'tp')
- grad_b_query: float32 [1024], P(('tp', 'fsdp'))
- grad_b_value: float32 [1024], P(('tp', 'fsdp'))
- grad_w_out: float32 [1024, 1024], P('tp', 'fsdp')
- grad_b_out: float32 [1024], P('fsdp')
- grad_gain_attn: float32 [1024], P('fsdp')
- grad_shift_attn: float32 [1024], P('fsdp')
- grad_w_up: float32 [1024, 4096], P('fsdp', 'tp')
- grad_b_up: float32 [4096], P(('tp', 'fsdp'))
- grad_w_down: float32 [4096, 1024], P('tp', 'fsdp')
- grad_b_down: float32 [1024], P('fsdp')
- grad_gain_ffn: float32 [1024], P('fsdp')
- grad_shift_ffn: float32 [1024], P('fsdp')
Inputs may be any that keep to these rules, and one draw needn't show every extreme that they name: Slots 0 to lengths - 1 of a sequence are valid. One sequence has exactly 512 valid slots and one exactly 128.
All inputs are finite; a program needn't handle non-finite values.
Results may differ from a plain program's by a relative error of at most 0.024.
Values may be sent and summed in bfloat16 or wider, within the bound.
No kernel may reach another device: no remote copies, remote signals or barrier semaphores. Data moves between devices by JAX's collectives and lax.ppermute only.
A program may use at most 128 MiB of HBM per device.

v0:
```python
import jax
import jax.numpy as jnp
from jax import lax
from jax.sharding import PartitionSpec as P

DH = 64


EPSILON = 1e-12
MASKED = -1000000000.0


def normalize(row_data, gain_vec, shift_vec):
    row_mean = jnp.mean(row_data, axis=-1, keepdims=True)
    centered = row_data - row_mean
    row_var = jnp.mean(centered * centered, axis=-1, keepdims=True)
    return centered * lax.rsqrt(row_var + EPSILON) * gain_vec + shift_vec


def gelu_exact(inner):
    return jax.nn.gelu(inner, approximate=False)


def split_heads(matrix):
    return matrix.reshape(matrix.shape[0], matrix.shape[1] // DH, DH)


def head_scores(query_heads, key_heads, key_mask):
    raw_scores = jnp.einsum(
        "qhd,khd->hqk", query_heads, key_heads, preferred_element_type=jnp.float32
    ) * DH ** (-0.5)
    return jnp.where(key_mask[None, None, :], raw_scores, MASKED)


def attend(inputs):
    query_rows, key_rows, value_rows, key_mask = inputs
    scores = head_scores(split_heads(query_rows), split_heads(key_rows), key_mask)
    row_top = jnp.max(scores, axis=-1, keepdims=True)
    exp_scores = jnp.exp(scores - row_top)
    row_total = jnp.sum(exp_scores, axis=-1, keepdims=True)
    probs_low = (exp_scores / row_total).astype(jnp.bfloat16)
    mixed = jnp.einsum(
        "hqk,khd->qhd", probs_low, split_heads(value_rows), preferred_element_type=jnp.float32
    )
    return (mixed.reshape(query_rows.shape).astype(jnp.bfloat16), row_top + jnp.log(row_total))


def attend_back(inputs):
    query_rows, key_rows, value_rows, key_mask, log_total, grad_rows = inputs
    query_heads = split_heads(query_rows)
    key_heads = split_heads(key_rows)
    value_heads = split_heads(value_rows)
    grad_heads = split_heads(grad_rows)
    scores = head_scores(query_heads, key_heads, key_mask)
    attn_probs = jnp.exp(scores - log_total)
    probs_low = attn_probs.astype(jnp.bfloat16)
    grad_probs = jnp.einsum(
        "qhd,khd->hqk", grad_heads, value_heads, preferred_element_type=jnp.float32
    ).astype(jnp.bfloat16)
    delta_sum = jnp.sum(attn_probs * grad_probs, axis=-1, keepdims=True)
    grad_scores = (attn_probs * (grad_probs - delta_sum)).astype(jnp.bfloat16)
    scale_factor = DH ** (-0.5)
    grad_query = (
        jnp.einsum("hqk,khd->qhd", grad_scores, key_heads, preferred_element_type=jnp.float32)
        * scale_factor
    ).astype(jnp.bfloat16)
    grad_key = (
        jnp.einsum("hqk,qhd->khd", grad_scores, query_heads, preferred_element_type=jnp.float32)
        * scale_factor
    )
    grad_value = jnp.einsum(
        "hqk,qhd->khd", probs_low, grad_heads, preferred_element_type=jnp.float32
    )
    return (
        grad_query.reshape(query_rows.shape),
        grad_key.reshape(key_rows.shape),
        grad_value.reshape(value_rows.shape),
    )


def forward_pass(params, layer_in, lengths):
    full = (
        lax.all_gather(params[0], "fsdp", axis=0, tiled=True),
        lax.all_gather(params[1], "fsdp", axis=0, tiled=True),
        lax.all_gather(params[2], "fsdp", axis=0, tiled=True),
        lax.all_gather(params[3], "fsdp", axis=0, tiled=True),
        lax.all_gather(params[4], "fsdp", axis=0, tiled=True),
        lax.all_gather(params[5], "fsdp", axis=1, tiled=True),
        lax.all_gather(params[6], "fsdp", axis=0, tiled=True),
        lax.all_gather(params[7], "fsdp", axis=0, tiled=True),
        lax.all_gather(params[8], "fsdp", axis=0, tiled=True),
        lax.all_gather(params[9], "fsdp", axis=0, tiled=True),
        lax.all_gather(params[10], "fsdp", axis=0, tiled=True),
        lax.all_gather(params[11], "fsdp", axis=1, tiled=True),
        lax.all_gather(params[12], "fsdp", axis=0, tiled=True),
        lax.all_gather(params[13], "fsdp", axis=0, tiled=True),
        lax.all_gather(params[14], "fsdp", axis=0, tiled=True),
    )
    (
        query_full,
        key_full,
        value_full,
        query_bias,
        value_bias,
        out_full,
        out_bias,
        gain_one,
        shift_one,
        up_full,
        up_bias,
        down_full,
        down_bias,
        gain_two,
        shift_two,
    ) = full
    seq_count, local_slots, model_width = layer_in.shape
    gathered = lax.all_gather(layer_in, "tp", axis=1, tiled=True)
    ctx_slots = gathered.shape[1]
    flat_in = gathered.reshape(seq_count * ctx_slots, model_width)
    queries = (
        jnp.dot(flat_in, query_full, preferred_element_type=jnp.float32) + query_bias
    ).astype(jnp.bfloat16)
    keys_own = jnp.dot(flat_in, key_full, preferred_element_type=jnp.float32).astype(jnp.bfloat16)
    values_own = (
        jnp.dot(flat_in, value_full, preferred_element_type=jnp.float32) + value_bias
    ).astype(jnp.bfloat16)
    head_width = queries.shape[1]
    keys_all, values_all = (
        lax.all_gather(
            keys_own.reshape(seq_count, ctx_slots, head_width), "ctx", axis=1, tiled=True
        ),
        lax.all_gather(
            values_own.reshape(seq_count, ctx_slots, head_width), "ctx", axis=1, tiled=True
        ),
    )
    key_valid = (
        lax.broadcasted_iota(jnp.int32, (seq_count, keys_all.shape[1]), 1) < lengths[:, None]
    )
    query_seqs = queries.reshape(seq_count, ctx_slots, head_width)
    attn_low, log_total = lax.map(attend, (query_seqs, keys_all, values_all, key_valid))
    attn_flat = attn_low.reshape(seq_count * ctx_slots, head_width)
    proj_part = jnp.dot(attn_flat, out_full, preferred_element_type=jnp.float32).reshape(
        seq_count, ctx_slots, model_width
    )
    projected = (
        lax.psum_scatter(
            proj_part.astype(jnp.bfloat16), "tp", scatter_dimension=1, tiled=True
        ).astype(jnp.float32)
        + out_bias
    )
    resid_one = layer_in.astype(jnp.float32) + projected
    normed_one = normalize(resid_one, gain_one, shift_one)
    normed_low = normed_one.astype(jnp.bfloat16)
    normed_all = lax.all_gather(normed_low, "tp", axis=1, tiled=True).reshape(
        seq_count * ctx_slots, model_width
    )
    hidden_pre = jnp.dot(normed_all, up_full, preferred_element_type=jnp.float32) + up_bias
    hidden = gelu_exact(hidden_pre).astype(jnp.bfloat16)
    down_part = jnp.dot(hidden, down_full, preferred_element_type=jnp.float32).reshape(
        seq_count, ctx_slots, model_width
    )
    ffn_out = (
        lax.psum_scatter(
            down_part.astype(jnp.bfloat16), "tp", scatter_dimension=1, tiled=True
        ).astype(jnp.float32)
        + down_bias
    )
    resid_two = normed_one + ffn_out
    layer_out = normalize(resid_two, gain_two, shift_two)
    saved = (
        full,
        flat_in,
        query_seqs,
        keys_all,
        values_all,
        key_valid,
        log_total,
        attn_flat,
        resid_one,
        normed_all,
        hidden_pre,
        hidden,
        resid_two,
    )
    return (layer_out, saved)


def backward_pass(saved, cotangent, lengths):
    (
        full,
        flat_in,
        query_seqs,
        keys_all,
        values_all,
        key_valid,
        log_total,
        attn_flat,
        resid_one,
        normed_all,
        hidden_pre,
        hidden,
        resid_two,
    ) = saved
    (
        query_full,
        key_full,
        value_full,
        query_bias,
        value_bias,
        out_full,
        out_bias,
        gain_one,
        shift_one,
        up_full,
        up_bias,
        down_full,
        down_bias,
        gain_two,
        shift_two,
    ) = full
    seq_count, local_slots, model_width = cotangent.shape
    ctx_slots = query_seqs.shape[1]
    head_width = query_seqs.shape[2]
    slot_index = (
        lax.axis_index("ctx") * ctx_slots
        + lax.axis_index("tp") * local_slots
        + lax.broadcasted_iota(jnp.int32, (seq_count, local_slots), 1)
    )
    row_valid = (slot_index < lengths[:, None]).astype(jnp.float32)
    grad_out = cotangent.astype(jnp.float32) * row_valid[:, :, None]
    norm_two, pull_two = jax.vjp(normalize, resid_two, gain_two, shift_two)
    grad_resid_two, grad_gain_two, grad_shift_two = pull_two(grad_out)
    grad_ffn_low = grad_resid_two.astype(jnp.bfloat16)
    grad_down_bias = jnp.sum(grad_ffn_low, axis=(0, 1), dtype=jnp.float32)
    grad_ffn_all = lax.all_gather(grad_ffn_low, "tp", axis=1, tiled=True).reshape(
        seq_count * ctx_slots, model_width
    )
    grad_down = jnp.einsum("rf,rd->fd", hidden, grad_ffn_all, preferred_element_type=jnp.float32)
    grad_hidden = jnp.einsum(
        "rd,fd->rf", grad_ffn_all, down_full, preferred_element_type=jnp.float32
    )
    gelu_value, gelu_pull = jax.vjp(gelu_exact, hidden_pre)
    grad_pre_low = gelu_pull(grad_hidden)[0].astype(jnp.bfloat16)
    grad_up_bias = jnp.sum(grad_pre_low, axis=0, dtype=jnp.float32)
    grad_up = jnp.einsum("rd,rf->df", normed_all, grad_pre_low, preferred_element_type=jnp.float32)
    normed_part = jnp.einsum(
        "rf,df->rd", grad_pre_low, up_full, preferred_element_type=jnp.float32
    ).reshape(seq_count, ctx_slots, model_width)
    grad_normed = (
        lax.psum_scatter(
            normed_part.astype(jnp.bfloat16), "tp", scatter_dimension=1, tiled=True
        ).astype(jnp.float32)
        + grad_resid_two
    )
    norm_one, pull_one = jax.vjp(normalize, resid_one, gain_one, shift_one)
    grad_resid_one, grad_gain_one, grad_shift_one = pull_one(grad_normed)
    grad_proj_low = grad_resid_one.astype(jnp.bfloat16)
    grad_out_bias = jnp.sum(grad_proj_low, axis=(0, 1), dtype=jnp.float32)
    grad_proj_all = lax.all_gather(grad_proj_low, "tp", axis=1, tiled=True).reshape(
        seq_count * ctx_slots, model_width
    )
    grad_out_w = jnp.einsum(
        "re,rd->ed", attn_flat, grad_proj_all, preferred_element_type=jnp.float32
    )
    grad_attn = (
        jnp.einsum("rd,ed->re", grad_proj_all, out_full, preferred_element_type=jnp.float32)
        .astype(jnp.bfloat16)
        .reshape(seq_count, ctx_slots, head_width)
    )
    grad_query_seqs, key_part, value_part = lax.map(
        attend_back, (query_seqs, keys_all, values_all, key_valid, log_total, grad_attn)
    )
    key_sum, value_sum = (
        lax.psum_scatter(
            key_part.astype(jnp.bfloat16), "ctx", scatter_dimension=1, tiled=True
        ).astype(jnp.float32),
        lax.psum_scatter(
            value_part.astype(jnp.bfloat16), "ctx", scatter_dimension=1, tiled=True
        ).astype(jnp.float32),
    )
    grad_key = key_sum.astype(jnp.bfloat16).reshape(seq_count * ctx_slots, head_width)
    grad_value = value_sum.astype(jnp.bfloat16).reshape(seq_count * ctx_slots, head_width)
    grad_query = grad_query_seqs.reshape(seq_count * ctx_slots, head_width)
    grad_query_bias = jnp.sum(grad_query, axis=0, dtype=jnp.float32)
    grad_value_bias = jnp.sum(grad_value, axis=0, dtype=jnp.float32)
    grad_query_w = jnp.einsum("rd,re->de", flat_in, grad_query, preferred_element_type=jnp.float32)
    grad_key_w = jnp.einsum("rd,re->de", flat_in, grad_key, preferred_element_type=jnp.float32)
    grad_value_w = jnp.einsum("rd,re->de", flat_in, grad_value, preferred_element_type=jnp.float32)
    input_part = (
        jnp.einsum("re,de->rd", grad_query, query_full, preferred_element_type=jnp.float32)
        + jnp.einsum("re,de->rd", grad_key, key_full, preferred_element_type=jnp.float32)
        + jnp.einsum("re,de->rd", grad_value, value_full, preferred_element_type=jnp.float32)
    ).reshape(seq_count, ctx_slots, model_width)
    input_grad = (
        lax.psum_scatter(
            input_part.astype(jnp.bfloat16), "tp", scatter_dimension=1, tiled=True
        ).astype(jnp.float32)
        + grad_resid_one
    ).astype(jnp.bfloat16)
    shards = (
        lax.psum_scatter(
            grad_query_w.astype(jnp.bfloat16), "fsdp", scatter_dimension=0, tiled=True
        ).astype(jnp.float32),
        lax.psum_scatter(
            grad_key_w.astype(jnp.bfloat16), "fsdp", scatter_dimension=0, tiled=True
        ).astype(jnp.float32),
        lax.psum_scatter(
            grad_value_w.astype(jnp.bfloat16), "fsdp", scatter_dimension=0, tiled=True
        ).astype(jnp.float32),
        lax.psum_scatter(
            grad_query_bias.astype(jnp.bfloat16), "fsdp", scatter_dimension=0, tiled=True
        ).astype(jnp.float32),
        lax.psum_scatter(
            grad_value_bias.astype(jnp.bfloat16), "fsdp", scatter_dimension=0, tiled=True
        ).astype(jnp.float32),
        lax.psum_scatter(
            grad_out_w.astype(jnp.bfloat16), "fsdp", scatter_dimension=1, tiled=True
        ).astype(jnp.float32),
        lax.psum_scatter(
            grad_out_bias.astype(jnp.bfloat16), "fsdp", scatter_dimension=0, tiled=True
        ).astype(jnp.float32),
        lax.psum_scatter(grad_gain_one, "fsdp", scatter_dimension=0, tiled=True).astype(
            jnp.float32
        ),
        lax.psum_scatter(grad_shift_one, "fsdp", scatter_dimension=0, tiled=True).astype(
            jnp.float32
        ),
        lax.psum_scatter(
            grad_up.astype(jnp.bfloat16), "fsdp", scatter_dimension=0, tiled=True
        ).astype(jnp.float32),
        lax.psum_scatter(
            grad_up_bias.astype(jnp.bfloat16), "fsdp", scatter_dimension=0, tiled=True
        ).astype(jnp.float32),
        lax.psum_scatter(
            grad_down.astype(jnp.bfloat16), "fsdp", scatter_dimension=1, tiled=True
        ).astype(jnp.float32),
        lax.psum_scatter(
            grad_down_bias.astype(jnp.bfloat16), "fsdp", scatter_dimension=0, tiled=True
        ).astype(jnp.float32),
        lax.psum_scatter(grad_gain_two, "fsdp", scatter_dimension=0, tiled=True).astype(
            jnp.float32
        ),
        lax.psum_scatter(grad_shift_two, "fsdp", scatter_dimension=0, tiled=True).astype(
            jnp.float32
        ),
    )
    split_sums = (
        lax.psum(shards[0].astype(jnp.bfloat16), "ctx").astype(jnp.float32),
        lax.psum(shards[1].astype(jnp.bfloat16), "ctx").astype(jnp.float32),
        lax.psum(shards[2].astype(jnp.bfloat16), "ctx").astype(jnp.float32),
        lax.psum(shards[3].astype(jnp.bfloat16), "ctx").astype(jnp.float32),
        lax.psum(shards[4].astype(jnp.bfloat16), "ctx").astype(jnp.float32),
        lax.psum(shards[5].astype(jnp.bfloat16), "ctx").astype(jnp.float32),
        lax.psum(shards[9].astype(jnp.bfloat16), "ctx").astype(jnp.float32),
        lax.psum(shards[10].astype(jnp.bfloat16), "ctx").astype(jnp.float32),
        lax.psum(shards[11].astype(jnp.bfloat16), "ctx").astype(jnp.float32),
    )
    vector_sums = lax.psum(
        (shards[6], shards[7], shards[8], shards[12], shards[13], shards[14]), ("ctx", "tp")
    )
    grads = (
        split_sums[0],
        split_sums[1],
        split_sums[2],
        split_sums[3],
        split_sums[4],
        split_sums[5],
        vector_sums[0],
        vector_sums[1],
        vector_sums[2],
        split_sums[6],
        split_sums[7],
        split_sums[8],
        vector_sums[3],
        vector_sums[4],
        vector_sums[5],
    )
    return (input_grad, grads)


def on_device(
    layer_in,
    lengths,
    cotangent,
    w_query,
    w_key,
    w_value,
    b_query,
    b_value,
    w_out,
    b_out,
    gain_attn,
    shift_attn,
    w_up,
    b_up,
    w_down,
    b_down,
    gain_ffn,
    shift_ffn,
):
    params = (
        w_query,
        w_key,
        w_value,
        b_query,
        b_value,
        w_out,
        b_out,
        gain_attn,
        shift_attn,
        w_up,
        b_up,
        w_down,
        b_down,
        gain_ffn,
        shift_ffn,
    )
    layer_out, saved = forward_pass(params, layer_in, lengths)
    fresh = lax.optimization_barrier((params, layer_in))
    second_out, saved_back = forward_pass(fresh[0], fresh[1], lengths)
    input_grad, grads = backward_pass(saved_back, cotangent, lengths)
    return (layer_out.astype(jnp.bfloat16), input_grad) + grads


def solution(mesh):
    return jax.shard_map(
        on_device,
        mesh=mesh,
        in_specs=(
            P("fsdp", ("ctx", "tp"), None),
            P("fsdp"),
            P("fsdp", ("ctx", "tp"), None),
            P("fsdp", "tp"),
            P("fsdp", "tp"),
            P("fsdp", "tp"),
            P(("tp", "fsdp")),
            P(("tp", "fsdp")),
            P("tp", "fsdp"),
            P("fsdp"),
            P("fsdp"),
            P("fsdp"),
            P("fsdp", "tp"),
            P(("tp", "fsdp")),
            P("tp", "fsdp"),
            P("fsdp"),
            P("fsdp"),
            P("fsdp"),
        ),
        out_specs=(
            P("fsdp", ("ctx", "tp"), None),
            P("fsdp", ("ctx", "tp"), None),
            P("fsdp", "tp"),
            P("fsdp", "tp"),
            P("fsdp", "tp"),
            P(("tp", "fsdp")),
            P(("tp", "fsdp")),
            P("tp", "fsdp"),
            P("fsdp"),
            P("fsdp"),
            P("fsdp"),
            P("fsdp", "tp"),
            P(("tp", "fsdp")),
            P("tp", "fsdp"),
            P("fsdp"),
            P("fsdp"),
            P("fsdp"),
        ),
        check_vma=False,
    )
```

profile of v0, /device:TPU:0, one launch (start us, length us, event | category | flops | bytes accessed | tf_op | source)
XLA Modules:
  0.0 906.7 jit_solution(14402246670868099785)
XLA Ops:
  12.5 8.3 all-reduce.15
  20.9 6.7 all_gather.141
  27.6 31.2 %all-gather.40.cloned.1.call-done = bf16[4,256,1024]{2,1,0:T(8,128)(2,1)} async-done(((bf16[4,64,1024]{2,1,0:T(8,128)(2,1)}), bf16[4,256,1024]{2,1,0:T(8,128)(2,1)}) %all-gather.40.cloned.1.call-update) | async-done | bytes 2097168 | tf_op jit(solution)/shard_map/all_gather | solution.py:117
  58.8 2.3 fusion.54
  62.3 7.1 all_gather.137
  70.2 2.4 convolution_convert_fusion.10
  73.7 7.3 all_gather.139
  81.0 7.3 all_gather.144
  88.3 2.3 fusion.53
  91.7 14.1 %all-gather.42.cloned.1.call-done = bf16[4,512,256]{1,2,0:T(8,128)(2,1)} async-done(((bf16[4,256,256]{1,2,0:T(8,128)(2,1)}), bf16[4,512,256]{1,2,0:T(8,128)(2,1)}) %all-gather.42.cloned.1.call-update) | async-done | bytes 1048592 | tf_op jit(solution)/shard_map/all_gather | solution.py:129
  105.8 18.3 %while.37 = (s32[]{:T(128)}, bf16[4,256,256]{1,2,0:T(8,128)(2,1)S(1)}, f32[4,4,256,1]{2,1,3,0:T(4,128)}, bf16[4,512,256]{1,2,0:T(8,128)(2,1)}, pred[4,512]{1,0:T...) while((s32[]{:T(128)}, ...), condition=%wide.region_13.14_spmd, body=%wide.region_10.13_spmd.sunk | while | flops 140573696 | bytes 8686693 | solution.py:140
  126.9 5.1 all-gather.7
  132.0 5.1 all-gather.8
  137.1 5.2 all-gather.9
  142.3 27.8 %reduce-scatter.19.cloned.1.call-done = bf16[4,64,1024]{2,1,0:T(8,128)(2,1)} async-done(((bf16[4,256,1024]{2,1,0:T(8,128)(2,1)}), bf16[4,64,1024]{2,1,0:T(8,128)(2,1)}) %reduce-scatter.19.cloned.1.call-update) | async-done | bytes 524304 | tf_op jit(solution)/shard_map/reduce_scatter | solution.py:146
  175.6 5.6 all-gather.10
  181.2 38.6 %all-gather.46.cloned.1.call-done = bf16[4,256,1024]{2,1,0:T(8,128)(2,1)} async-done(((bf16[4,64,1024]{2,1,0:T(8,128)(2,1)}), bf16[4,256,1024]{2,1,0:T(8,128)(2,1)}) %all-gather.46.cloned.1.call-update) | async-done | bytes 2097168 | tf_op jit(solution)/shard_map/all_gather | solution.py:154
  219.7 14.9 %multiply_convert_fusion = (bf16[1024,1024]{1,0:T(8,128)(2,1)}, f32[1024,1024]{1,0:T(8,128)}, f32[1024,1024]{1,0:T(8,128)}) fusion(f32[1024]{0:T(1024)S(1)} %bitcast.283, bf16[1024,1024]{1,0:T(8,128)(2,1)} %bitcast.289, bf16[1024,1024]{1,0:T(8,128)(2,1)} %all-gather.48.cloned.1.call-done), kind=kOutput, calls=%fused_computation.63 | convolution fusion | flops 2216689664 | bytes 14684160 | tf_op jit(solution)/shard_map/dot_general | solution.py:157
  234.6 8.0 all-gather.50.cloned.1.call-done
  242.7 5.9 convolution_convert_fusion.6
  248.7 5.2 all-gather.12
  253.9 5.1 all-gather.11
  259.1 33.4 %reduce-scatter.21.cloned.1.call-done = bf16[4,64,1024]{2,1,0:T(8,128)(2,1)} async-done(((bf16[4,256,1024]{2,1,0:T(8,128)(2,1)}), bf16[4,64,1024]{2,1,0:T(8,128)(2,1)}) %reduce-scatter.21.cloned.1.call-update) | async-done | bytes 524304 | tf_op jit(solution)/shard_map/reduce_scatter | solution.py:163
  297.1 44.6 %all-gather.52.cloned.1.call-done = bf16[4,256,1024]{2,1,0:T(8,128)(2,1)} async-done(((bf16[4,64,1024]{2,1,0:T(8,128)(2,1)}), bf16[4,256,1024]{2,1,0:T(8,128)(2,1)}) %all-gather.52.cloned.1.call-update) | async-done | bytes 2097168 | tf_op jit(solution)/shard_map/all_gather | solution.py:235
  341.7 9.1 %fusion.98 = (bf16[1024]{0:T(1024)(128)(2,1)}, bf16[1024,1024]{1,0:T(8,128)(2,1)S(1)}) fusion(f32[1024,1024]{1,0:T(8,128)} %get-tuple-element.339, f32[1024,1024]{1,0:T(8,128)} %get-tuple-element.352, f32[1024]{0:T(1024)S(1)} %bitcast.284, bf16[1024,1024]{1,0:T(8,128)(2,1)} %bitcast.291, bf16[1024,1024]{1,0:T(8,128)(2,1)} %all-gather.50.cloned.1.call-done), kind=kOutput, calls=%fused_computation.206 | convolution fusion | flops 2164259840 | bytes 14686208 | tf_op jit(solution)/shard_map/rd,fd->rf/dot_general | solution.py:239
  350.8 3.7 convolution_convert_fusion.5
  354.6 42.5 %reduce-scatter.23.cloned.1.call-done = bf16[4,64,1024]{2,1,0:T(8,128)(2,1)} async-done(((bf16[4,256,1024]{2,1,0:T(8,128)(2,1)}), bf16[4,64,1024]{2,1,0:T(8,128)(2,1)}) %reduce-scatter.23.cloned.1.call-update) | async-done | bytes 524304 | tf_op jit(solution)/shard_map/reduce_scatter | solution.py:250
  404.4 44.1 %all-gather.54.cloned.1.call-done = bf16[4,256,1024]{2,1,0:T(8,128)(2,1)} async-done(((bf16[4,64,1024]{2,1,0:T(8,128)(2,1)}), bf16[4,256,1024]{2,1,0:T(8,128)(2,1)}) %all-gather.54.cloned.1.call-update) | async-done | bytes 2097168 | tf_op jit(solution)/shard_map/all_gather | solution.py:259
  448.5 3.1 convolution_convert_fusion.9
  452.5 47.5 %while.38 = (s32[]{:T(128)}, bf16[4,256,256]{1,2,0:T(8,128)(2,1)}, bf16[4,512,256]{2,1,0:T(8,128)(2,1)}, bf16[4,512,256]{2,1,0:T(8,128)(2,1)}, bf16[4,512,256]{1...) while((s32[]{:T(128)}, bf16[4,256,256]{1,2,0:T(8,128)(2,1)}, ...), condition=%wide.region_27.28_spmd, body=%wide.region_25.27_spmd.sunk | while | flops 342227968 | bytes 19815072 | solution.py:270
  500.1 7.4 all_gather.123
  507.5 2.3 convolution_convert_fusion.11
  511.4 7.5 all_gather.118
  520.6 10.7 %all-reduce.14 = (bf16[256]{0:T(256)(128)(2,1)S(1)}, bf16[256]{0:T(256)(128)(2,1)S(1)}, bf16[256]{0:T(256)(128)(2,1)S(1)}, bf16[256]{0:T(256)(128)(2,1)S(1)}, bf...) all-reduce(bf16[256]{0:T(256)(128)(2,1)S(1)} %dynamic-update-slice,, ...), channel_id=1, replica_groups=mesh['fsdp'=4,'ctx'=2,'tp'=4] {'fsdp'}, use_global_device_ids=true, to_apply=%add | all-reduce | flops 8192 | bytes 32768
  531.3 2.3 fusion.51
  534.8 6.8 all_gather.121
  541.5 7.3 all_gather.125
  548.9 2.3 fusion.52
  551.2 14.7 %all-gather.30.cloned.1.call-done = bf16[4,512,256]{1,2,0:T(8,128)(2,1)} async-done(((bf16[4,256,256]{1,2,0:T(8,128)(2,1)}), bf16[4,512,256]{1,2,0:T(8,128)(2,1)}) %all-gather.30.cloned.1.call-update) | async-done | bytes 1048592 | tf_op jit(solution)/shard_map/all_gather | solution.py:132
  566.0 12.7 %while.36 = (s32[]{:T(128)}, bf16[4,256,256]{1,2,0:T(8,128)(2,1)S(1)}, bf16[4,512,256]{1,2,0:T(8,128)(2,1)}, pred[4,512]{1,0:T(4,128)(4,1)S(1)}, bf16[4,256,256]...) while((s32[]{:T(128)}, bf16[4,256,256]{1,2,0:T(8,128)(2,1)S(1)}, ...), condition=%wide.region_3.4_spmd, body=%wide.region_0.3_spmd.sunk | while | flops 206112768 | bytes 3024989 | solution.py:140
  580.9 6.1 convolution_convert_fusion.3
  587.1 5.4 convolution_convert_fusion.4
  592.5 3.3 fusion.50
  597.9 3.2 fusion.48
  601.3 3.2 fusion.49
  606.0 5.1 all-gather
  611.0 5.1 all-gather.1
  616.1 5.2 all-gather.2
  621.3 13.7 %reduce-scatter.15.cloned.1.call-done = bf16[4,64,1024]{2,1,0:T(8,128)(2,1)} async-done(((bf16[4,256,1024]{2,1,0:T(8,128)(2,1)}), bf16[4,64,1024]{2,1,0:T(8,128)(2,1)}) %reduce-scatter.15.cloned.1.call-update) | async-done | bytes 524304 | tf_op jit(solution)/shard_map/reduce_scatter | solution.py:146
  640.0 28.0 %reduce-scatter.41.cloned.1.call-done = bf16[1024,256]{1,0:T(8,128)(2,1)} async-done(((bf16[1024,1024]{1,0:T(8,128)(2,1)}), bf16[1024,256]{1,0:T(8,128)(2,1)}) %reduce-scatter.41.cloned.1.call-update) | async-done | bytes 524304 | tf_op jit(solution)/shard_map/reduce_scatter | solution.py:334
  668.0 33.6 %reduce-scatter.39.cloned.1.call-done = bf16[256,1024]{1,0:T(8,128)(2,1)} async-done(((bf16[1024,1024]{1,0:T(8,128)(2,1)}), bf16[256,1024]{1,0:T(8,128)(2,1)}) %reduce-scatter.39.cloned.1.call-update) | async-done | bytes 524304 | tf_op jit(solution)/shard_map/reduce_scatter | solution.py:328
  701.6 24.0 %reduce-scatter.37.cloned.1.call-done = bf16[256,256]{1,0:T(8,128)(2,1)} async-done(((bf16[256,1024]{1,0:T(8,128)(2,1)}), bf16[256,256]{1,0:T(8,128)(2,1)}) %reduce-scatter.37.cloned.1.call-update) | async-done | bytes 131088 | tf_op jit(solution)/shard_map/reduce_scatter | solution.py:316
  725.6 24.6 %reduce-scatter.31.cloned.1.call-done = bf16[256,256]{1,0:T(8,128)(2,1)} async-done(((bf16[1024,256]{1,0:T(8,128)(2,1)}), bf16[256,256]{1,0:T(8,128)(2,1)}) %reduce-scatter.31.cloned.1.call-update) | async-done | bytes 131088 | tf_op jit(solution)/shard_map/reduce_scatter | solution.py:301
  750.2 24.6 %reduce-scatter.33.cloned.1.call-done = bf16[256,256]{1,0:T(8,128)(2,1)} async-done(((bf16[1024,256]{1,0:T(8,128)(2,1)}), bf16[256,256]{1,0:T(8,128)(2,1)}) %reduce-scatter.33.cloned.1.call-update) | async-done | bytes 131088 | tf_op jit(solution)/shard_map/reduce_scatter | solution.py:304
  774.8 24.6 %reduce-scatter.35.cloned.1.call-done = bf16[256,256]{1,0:T(8,128)(2,1)} async-done(((bf16[1024,256]{1,0:T(8,128)(2,1)}), bf16[256,256]{1,0:T(8,128)(2,1)}) %reduce-scatter.35.cloned.1.call-update) | async-done | bytes 131088 | tf_op jit(solution)/shard_map/reduce_scatter | solution.py:307
  803.8 5.1 all-gather.3
  808.9 16.6 %fusion.44 = bf16[1024,1024]{1,0:T(8,128)(2,1)} fusion(bf16[1024,1024]{1,0:T(8,128)(2,1)} %all-gather.38.cloned.1.call-done, f32[1024]{0:T(1024)S(1)} %bitcast.285, bf16[1024,1024]{1,0:T(8,128)(2,1)} %bitcast.297, bf16[1024,1024]{1,0:T(8,128)(2,1)} %all-gather.36.cloned.1.call-done), kind=kOutput, calls=%fused_computation.100 | convolution fusion | flops 4365221888 | bytes 8392704 | tf_op jit(solution)/shard_map/dot_general | solution.py:159
  827.0 5.1 all-gather.4
  832.1 5.1 all-gather.5
  837.1 5.1 all-gather.6
  842.4 5.3 all-reduce.16
  849.5 24.1 %all-reduce.13 = (f32[256]{0:T(256)}, f32[256]{0:T(256)}, f32[256]{0:T(256)}, f32[256]{0:T(256)}, f32[256]{0:T(256)}, /*index=5*/f32[256]{0:T(256)}) all-reduce(f32[256]{0:T(256)S(1)} %get-tuple-element.358, f32[256]{0:T(256)S(1)} %get-tuple-element.357, ...), channel_id=1, replica_groups=mesh['fsdp'=4,'ctx'=2,'tp'=4] {'ctx','tp'}, use_global_device_ids=true, to_apply=%region_47.48 | all-reduce | flops 1536 | bytes 12288 | tf_op jit(solution)/shard_map/psum | solution.py:358
  885.5 7.9 reduce-scatter.17.cloned.1.call-done
  896.7 2.7 add_convert_fusion.3
  (411 shorter events, 143.6 us)
Async XLA Ops:
  8.0 50.8 %all-gather.40.cloned.1.call-start = ((), (), s32[]{:S(2)}) async-start(), calls=%async_computation.22 | async-start | bytes 2621440 | tf_op jit(solution)/shard_map/all_gather | solution.py:117
  8.8 82.9 %all-gather.44.cloned.1.call-start = ((), (), s32[]{:S(2)}) async-start(), calls=%async_computation.24 | async-start | bytes 1572864 | tf_op jit(solution)/shard_map/all_gather | solution.py:132
  27.6 34.6 %copy-start.8 = (bf16[1024,256]{1,0:T(8,128)(2,1)}, bf16[1024,256]{1,0:T(8,128)(2,1)S(1)}, u32[]{:S(2)}) copy-start(bf16[1024,256]{1,0:T(8,128)(2,1)S(1)} %all_gather.141) | copy-start | bytes 1572868
  62.2 11.5 %copy-start.21 = (bf16[256,256]{1,0:T(8,128)(2,1)S(1)}, bf16[256,256]{1,0:T(8,128)(2,1)}, u32[]{:S(2)}) copy-start(bf16[256,256]{1,0:T(8,128)(2,1)} %param.27) | copy-start | bytes 393220
  62.2 43.6 %all-gather.42.cloned.1.call-start = ((), (), s32[]{:S(2)}) async-start(), calls=%async_computation.23 | async-start | bytes 1572864 | tf_op jit(solution)/shard_map/all_gather | solution.py:129
  70.2 10.8 %copy-start.23 = (bf16[256,256]{1,0:T(8,128)(2,1)S(1)}, bf16[256,256]{1,0:T(8,128)(2,1)}, u32[]{:S(2)}) copy-start(bf16[256,256]{1,0:T(8,128)(2,1)} %param.32) | copy-start | bytes 393220
  70.2 18.0 %copy-start.30 = (s32[4]{0:T(128)S(1)}, s32[4]{0:T(128)}, u32[]{:S(2)}) copy-start(s32[4]{0:T(128)} %param.25) | copy-start | bytes 52
  73.6 96.4 %reduce-scatter.19.cloned.1.call-start = ((), (), s32[]{:S(2)}) async-start(), calls=%async_computation.25 | async-start | bytes 2621440 | tf_op jit(solution)/shard_map/reduce_scatter | solution.py:146
  81.0 7.3 copy-start.12
  124.1 50.8 %copy-start.16 = (bf16[4,256,256]{1,2,0:T(8,128)(2,1)}, bf16[4,256,256]{1,2,0:T(8,128)(2,1)S(1)}, u32[]{:S(2)}) copy-start(bf16[4,256,256]{1,2,0:T(8,128)(2,1)S(1)} %get-tuple-element.164) | copy-start | bytes 1572868
  124.1 7.9 copy-start.39
  124.1 12.9 %copy-start.41 = (bf16[256]{0:T(256)(128)(2,1)S(1)}, bf16[256]{0:T(256)(128)(2,1)}, u32[]{:S(2)}) copy-start(bf16[256]{0:T(256)(128)(2,1)} %param.35) | copy-start | bytes 1540
  124.2 45.9 %copy-start = (bf16[4,64,1024]{2,1,0:T(8,128)(2,1)S(1)}, bf16[4,64,1024]{2,1,0:T(8,128)(2,1)}, u32[]{:S(2)}) copy-start(bf16[4,64,1024]{2,1,0:T(8,128)(2,1)} %param.24) | copy-start | bytes 1572868
  126.2 49.3 %copy-start.43 = (bf16[256]{0:T(256)(128)(2,1)S(1)}, bf16[256]{0:T(256)(128)(2,1)}, u32[]{:S(2)}) copy-start(bf16[256]{0:T(256)(128)(2,1)} %param.37) | copy-start | bytes 1540
  126.3 54.9 %all-gather.48.cloned.1.call-start = ((), (), s32[]{:S(2)}) async-start(), calls=%async_computation.27 | async-start | bytes 2621440 | tf_op jit(solution)/shard_map/all_gather | solution.py:92
  126.8 92.9 %all-gather.46.cloned.1.call-start = ((), (), s32[]{:S(2)}) async-start(), calls=%async_computation.26 | async-start | bytes 2621440 | tf_op jit(solution)/shard_map/all_gather | solution.py:154
  174.9 67.8 %all-gather.50.cloned.1.call-start = ((), (), s32[]{:S(2)}) async-start(), calls=%async_computation.28 | async-start | bytes 2621440 | tf_op jit(solution)/shard_map/all_gather | solution.py:94
  175.5 116.9 %reduce-scatter.21.cloned.1.call-start = ((), (), s32[]{:S(2)}) async-start(), calls=%async_computation.29 | async-start | bytes 2621440 | tf_op jit(solution)/shard_map/reduce_scatter | solution.py:163
  242.7 6.0 copy-start.45
  242.7 11.2 %copy-start.47 = (bf16[256]{0:T(256)(128)(2,1)S(1)}, bf16[256]{0:T(256)(128)(2,1)}, u32[]{:S(2)}) copy-start(bf16[256]{0:T(256)(128)(2,1)} %param.40) | copy-start | bytes 1540
  242.7 49.7 %copy-start.4 = (bf16[4,64,1024]{2,1,0:T(8,128)(2,1)S(1)}, bf16[4,64,1024]{2,1,0:T(8,128)(2,1)}, u32[]{:S(2)}) copy-start(bf16[4,64,1024]{2,1,0:T(8,128)(2,1)} %reduce-scatter.19.cloned.1.call-done) | copy-start | bytes 1572868
  248.6 45.7 %copy-start.15 = (bf16[4,64,1024]{2,1,0:T(8,128)(2,1)S(1)}, bf16[4,64,1024]{2,1,0:T(8,128)(2,1)}, u32[]{:S(2)}) copy-start(bf16[4,64,1024]{2,1,0:T(8,128)(2,1)} %param.26) | copy-start | bytes 1572868
  248.6 93.1 %all-gather.52.cloned.1.call-start = ((), (), s32[]{:S(2)}) async-start(), calls=%async_computation.30 | async-start | bytes 2621440 | tf_op jit(solution)/shard_map/all_gather | solution.py:235
  296.9 100.2 %reduce-scatter.23.cloned.1.call-start = ((), (), s32[]{:S(2)}) async-start(), calls=%async_computation.31 | async-start | bytes 2621440 | tf_op jit(solution)/shard_map/reduce_scatter | solution.py:250
  341.7 9.1 %copy-start.34 = (bf16[1024,1024]{1,0:T(8,128)(2,1)S(1)}, bf16[1024,1024]{1,0:T(8,128)(2,1)}, u32[]{:S(2)}) copy-start(bf16[1024,1024]{1,0:T(8,128)(2,1)} %all-gather.48.cloned.1.call-done) | copy-start | bytes 6291460
  354.5 94.0 %all-gather.54.cloned.1.call-start = ((), (), s32[]{:S(2)}) async-start(), calls=%async_computation.32 | async-start | bytes 2621440 | tf_op jit(solution)/shard_map/all_gather | solution.py:259
  403.6 103.9 %all-gather.28.cloned.1.call-start = ((), (), s32[]{:S(2)}) async-start(), calls=%async_computation.14 | async-start | bytes 2621440 | tf_op jit(solution)/shard_map/all_gather | solution.py:117
  404.3 115.0 %reduce-scatter.27.cloned.1.call-start = ((), (), s32[]{:S(2)}) async-start(), calls=%async_computation.34 | async-start | bytes 1572864 | tf_op jit(solution)/shard_map/reduce_scatter | solution.py:277
  500.0 10.9 %copy-start.35 = (bf16[64]{0:T(256)(128)(2,1)S(1)}, bf16[64]{0:T(256)(128)(2,1)}, u32[]{:S(2)}) copy-start(bf16[64]{0:T(256)(128)(2,1)} %param.31) | copy-start | bytes 388
  500.0 11.2 %copy-start.36 = (bf16[64]{0:T(256)(128)(2,1)S(1)}, bf16[64]{0:T(256)(128)(2,1)}, u32[]{:S(2)}) copy-start(bf16[64]{0:T(256)(128)(2,1)} %param.30) | copy-start | bytes 388
  500.0 11.4 %copy-start.20 = (bf16[256,256]{1,0:T(8,128)(2,1)S(1)}, bf16[256,256]{1,0:T(8,128)(2,1)}, u32[]{:S(2)}) copy-start(bf16[256,256]{1,0:T(8,128)(2,1)} %param.29) | copy-start | bytes 393220
  500.0 51.2 %all-gather.32.cloned.1.call-start = ((), (), s32[]{:S(2)}) async-start(), calls=%async_computation.16 | async-start | bytes 1572864 | tf_op jit(solution)/shard_map/all_gather | solution.py:129
  507.4 11.5 %copy-start.7 = (bf16[4,256,256]{1,2,0:T(8,128)(2,1)S(1)}, bf16[4,256,256]{1,2,0:T(8,128)(2,1)}, u32[]{:S(2)}) copy-start(bf16[4,256,256]{1,2,0:T(8,128)(2,1)} %get-tuple-element.174) | copy-start | bytes 1572868
  507.4 13.1 %copy-start.26 = (bf16[1024]{0:T(1024)(128)(2,1)S(1)}, bf16[1024]{0:T(1024)(128)(2,1)}, u32[]{:S(2)}) copy-start(bf16[1024]{0:T(1024)(128)(2,1)} %get-tuple-element.328) | copy-start | bytes 6148
  507.5 13.1 %copy-start.27 = (bf16[1024]{0:T(1024)(128)(2,1)S(1)}, bf16[1024]{0:T(1024)(128)(2,1)}, u32[]{:S(2)}) copy-start(bf16[1024]{0:T(1024)(128)(2,1)} %get-tuple-element.246) | copy-start | bytes 6148
  507.5 13.1 %copy-start.28 = (bf16[1024]{0:T(1024)(128)(2,1)S(1)}, bf16[1024]{0:T(1024)(128)(2,1)}, u32[]{:S(2)}) copy-start(bf16[1024]{0:T(1024)(128)(2,1)} %get-tuple-element.250) | copy-start | bytes 6148
  507.5 13.1 %copy-start.29 = (bf16[1024]{0:T(1024)(128)(2,1)S(1)}, bf16[1024]{0:T(1024)(128)(2,1)}, u32[]{:S(2)}) copy-start(bf16[1024]{0:T(1024)(128)(2,1)} %get-tuple-element.330) | copy-start | bytes 6148
  507.5 13.1 %copy-start.31 = (bf16[1024]{0:T(1024)(128)(2,1)S(1)}, bf16[1024]{0:T(1024)(128)(2,1)}, u32[]{:S(2)}) copy-start(bf16[1024]{0:T(1024)(128)(2,1)} %get-tuple-element.326) | copy-start | bytes 6148
  510.9 55.1 %all-gather.30.cloned.1.call-start = ((), (), s32[]{:S(2)}) async-start(), calls=%async_computation.15 | async-start | bytes 1572864 | tf_op jit(solution)/shard_map/all_gather | solution.py:132
  531.3 10.2 %copy-start.24 = (bf16[256,256]{1,0:T(8,128)(2,1)S(1)}, bf16[256,256]{1,0:T(8,128)(2,1)}, u32[]{:S(2)}) copy-start(bf16[256,256]{1,0:T(8,128)(2,1)} %param.32) | copy-start | bytes 393220
  534.7 63.2 %reduce-scatter.25.cloned.1.call-start = ((), (), s32[]{:S(2)}) async-start(), calls=%async_computation.33 | async-start | bytes 1572864 | tf_op jit(solution)/shard_map/reduce_scatter | solution.py:274
  548.8 86.2 %reduce-scatter.15.cloned.1.call-start = ((), (), s32[]{:S(2)}) async-start(), calls=%async_computation.17 | async-start | bytes 2621440 | tf_op jit(solution)/shard_map/reduce_scatter | solution.py:146
  580.8 6.3 copy-start.33
  580.8 87.2 %reduce-scatter.41.cloned.1.call-start = ((), (), s32[]{:S(2)}) async-start(), calls=%async_computation.41 | async-start | bytes 2621440 | tf_op jit(solution)/shard_map/reduce_scatter | solution.py:334
  587.0 114.6 %reduce-scatter.39.cloned.1.call-start = ((), (), s32[]{:S(2)}) async-start(), calls=%async_computation.40 | async-start | bytes 2621440 | tf_op jit(solution)/shard_map/reduce_scatter | solution.py:328
  592.5 133.1 %reduce-scatter.37.cloned.1.call-start = ((), (), s32[]{:S(2)}) async-start(), calls=%async_computation.39 | async-start | bytes 655360 | tf_op jit(solution)/shard_map/reduce_scatter | solution.py:316
  595.8 154.4 %reduce-scatter.31.cloned.1.call-start = ((), (), s32[]{:S(2)}) async-start(), calls=%async_computation.36 | async-start | bytes 655360 | tf_op jit(solution)/shard_map/reduce_scatter | solution.py:301
  597.5 177.4 %reduce-scatter.33.cloned.1.call-start = ((), (), s32[]{:S(2)}) async-start(), calls=%async_computation.37 | async-start | bytes 655360 | tf_op jit(solution)/shard_map/reduce_scatter | solution.py:304
  601.2 33.8 %copy-start.1 = (bf16[4,64,1024]{2,1,0:T(8,128)(2,1)S(1)}, bf16[4,64,1024]{2,1,0:T(8,128)(2,1)}, u32[]{:S(2)}) copy-start(bf16[4,64,1024]{2,1,0:T(8,128)(2,1)} %param.24) | copy-start | bytes 1572868
  601.2 198.2 %reduce-scatter.35.cloned.1.call-start = ((), (), s32[]{:S(2)}) async-start(), calls=%async_computation.38 | async-start | bytes 655360 | tf_op jit(solution)/shard_map/reduce_scatter | solution.py:307
  604.5 195.3 %copy-start.13 = (bf16[1024,256]{1,0:T(8,128)(2,1)S(1)}, bf16[1024,256]{1,0:T(8,128)(2,1)}, u32[]{:S(2)}) copy-start(bf16[1024,256]{1,0:T(8,128)(2,1)} %copy-done.12) | copy-start | bytes 1572868
  604.5 204.3 %all-gather.36.cloned.1.call-start = ((), (), s32[]{:S(2)}) async-start(), calls=%async_computation.19 | async-start | bytes 2621440 | tf_op jit(solution)/shard_map/all_gather | solution.py:92
  605.3 203.6 %all-gather.38.cloned.1.call-start = ((), (), s32[]{:S(2)}) async-start(), calls=%async_computation.20 | async-start | bytes 2621440 | tf_op jit(solution)/shard_map/all_gather | solution.py:94
  605.8 203.0 %all-gather.34.cloned.1.call-start = ((), (), s32[]{:S(2)}) async-start(), calls=%async_computation.18 | async-start | bytes 2621440 | tf_op jit(solution)/shard_map/all_gather | solution.py:154
  639.9 160.6 %copy-start.11 = (bf16[1024,256]{1,0:T(8,128)(2,1)S(1)}, bf16[1024,256]{1,0:T(8,128)(2,1)}, u32[]{:S(2)}) copy-start(bf16[1024,256]{1,0:T(8,128)(2,1)} %copy-done.10) | copy-start | bytes 1572868
  640.0 233.7 %all-reduce.20.cloned.1.call-start = ((), (), s32[]{:S(2)}) async-start(), calls=%async_computation.42 | async-start | bytes 3145728 | tf_op jit(solution)/shard_map/psum | solution.py:348
  799.5 84.0 %reduce-scatter.29.cloned.1.call-start = ((), (), s32[]{:S(2)}) async-start(), calls=%async_computation.35 | async-start | bytes 2621440 | tf_op jit(solution)/shard_map/reduce_scatter | solution.py:295
  803.7 89.7 %reduce-scatter.17.cloned.1.call-start = ((), (), s32[]{:S(2)}) async-start(), calls=%async_computation.21 | async-start | bytes 2621440 | tf_op jit(solution)/shard_map/reduce_scatter | solution.py:163
  808.9 16.6 %copy-start.46 = (bf16[256]{0:T(256)(128)(2,1)S(1)}, bf16[256]{0:T(256)(128)(2,1)}, u32[]{:S(2)}) copy-start(bf16[256]{0:T(256)(128)(2,1)} %param.39) | copy-start | bytes 1540
  808.9 16.6 %copy-start.48 = (bf16[256]{0:T(256)(128)(2,1)S(1)}, bf16[256]{0:T(256)(128)(2,1)}, u32[]{:S(2)}) copy-start(bf16[256]{0:T(256)(128)(2,1)} %param.40) | copy-start | bytes 1540
  808.9 16.7 %copy-start.49 = (bf16[256]{0:T(256)(128)(2,1)S(1)}, bf16[256]{0:T(256)(128)(2,1)}, u32[]{:S(2)}) copy-start(bf16[256]{0:T(256)(128)(2,1)} %param.41) | copy-start | bytes 1540
  825.5 58.0 %copy-start.6 = (f32[4,64,1024]{2,1,0:T(8,128)S(1)}, f32[4,64,1024]{2,1,0:T(8,128)}, u32[]{:S(2)}) copy-start(f32[4,64,1024]{2,1,0:T(8,128)} %copy-done.5) | copy-start | bytes 3145732
  825.5 67.9 %copy-start.3 = (bf16[4,64,1024]{2,1,0:T(8,128)(2,1)S(1)}, bf16[4,64,1024]{2,1,0:T(8,128)(2,1)}, u32[]{:S(2)}) copy-start(bf16[4,64,1024]{2,1,0:T(8,128)(2,1)} %reduce-scatter.15.cloned.1.call-done) | copy-start | bytes 1572868
  873.6 9.1 %copy-start.25 = (bf16[256,256]{1,0:T(8,128)(2,1)S(1)}, bf16[256,256]{1,0:T(8,128)(2,1)}, u32[]{:S(2)}) copy-start(bf16[256,256]{1,0:T(8,128)(2,1)} %get-tuple-element.323) | copy-start | bytes 393220
  (19 other events, 57.6 us)
Sparse Core Ops, SparseCore 0:
  10.4 48.3 all-gather.39
  62.3 20.0 all-gather.43
  84.5 21.2 all-gather.41
  126.4 43.6 reduce-scatter.18
  248.8 43.6 reduce-scatter.20
  403.7 44.7 all-gather.53
  450.1 44.4 all-gather.27
  500.1 19.1 reduce-scatter.26
  521.5 21.2 all-gather.31
  544.7 21.2 all-gather.29
  568.8 20.4 reduce-scatter.24
  591.4 43.5 reduce-scatter.14
  637.6 30.3 reduce-scatter.40
  670.4 31.1 reduce-scatter.38
  703.9 21.6 reduce-scatter.36
  728.5 21.6 reduce-scatter.30
  753.1 21.6 reduce-scatter.32
  777.8 21.6 reduce-scatter.34
  802.1 51.7 all-reduce.19
Sparse Core Ops, SparseCore 1:
  128.3 22.4 all-gather.47
  175.0 44.7 all-gather.45
  221.2 21.5 all-gather.49
  296.9 44.7 all-gather.51
  354.6 42.4 reduce-scatter.22
  606.9 22.8 all-gather.35
  631.1 22.6 all-gather.37
  655.8 45.5 all-gather.33
  803.8 43.6 reduce-scatter.28
  849.8 43.6 reduce-scatter.16
where the time goes:
time: 915 us; the launch traced here: 907 us
  waiting for transfers between devices  485 us (53%)
  blocking collectives  172 us (19%)
  matrix products  124 us (14%)
  local copies, waits for them, and re-layouts  57.8 us (6%)
  other arithmetic  47 us (5%)
  between operations  18.6 us (2%)
    all_gather x1, waiting for transfers between devices, backward_pass(): lax.all_gather(grad_ffn_low, 'tp', axis=1, tiled=True)  44.6 us
    all_gather x1, waiting for transfers between devices, backward_pass(): lax.all_gather(grad_proj_low, 'tp', axis=1, tiled=True)  44.1 us
    reduce_scatter x1, waiting for transfers between devices, backward_pass(): lax.psum_scatter(normed_part.astype(jnp.bfloat16), 'tp', scatter_dimensio...  42.5 us
    reduce_scatter x2, waiting for transfers between devices, forward_pass(): lax.psum_scatter(proj_part.astype(jnp.bfloat16), 'tp', scatter_dimension=...  41.5 us
    reduce_scatter x2, waiting for transfers between devices, forward_pass(): lax.psum_scatter(down_part.astype(jnp.bfloat16), 'tp', scatter_dimension=...  41.3 us
    all_gather x2, waiting for transfers between devices, forward_pass(): lax.all_gather(normed_low, 'tp', axis=1, tiled=True)  38.6 us
    reduce_scatter x1, waiting for transfers between devices, backward_pass(): lax.psum_scatter(grad_up.astype(jnp.bfloat16), 'fsdp', scatter_dimension=...  33.6 us
    all_gather x2, waiting for transfers between devices, forward_pass(): gathered = lax.all_gather(layer_in, 'tp', axis=1, tiled=True)  31.2 us
  transfers between devices with their start and end apart: 29, of which 19 were waited for; matrix products, arithmetic and copies ran while one was open for 19% of the time, Pallas kernels for 0%

commit v1 on v0

v1 whole, which is shorter than its diff:
```python
import functools

import jax
import jax.numpy as jnp
from jax import lax
from jax.experimental import pallas as pl
from jax.experimental.pallas import tpu as pltpu
from jax.sharding import Mesh, PartitionSpec as P

DH = 64
EPSILON = 1e-12
MASKED = -1000000000.0
SWAP = [(0, 1), (1, 0)]
F32 = jnp.float32
BF16 = jnp.bfloat16


def core_swap(array):
    return lax.ppermute(array, "core", SWAP)


def ctx_swap(array):
    return lax.ppermute(array, "ctx", SWAP)


def dot_nt(left, right):
    return lax.dot_general(left, right, (((1,), (1,)), ((), ())), preferred_element_type=F32)


def dot_nn(left, right):
    return lax.dot_general(left, right, (((1,), (0,)), ((), ())), preferred_element_type=F32)


def dot_tn(left, right):
    return lax.dot_general(left, right, (((0,), (0,)), ((), ())), preferred_element_type=F32)


def gather_rows(own):
    near = jnp.concatenate([own, core_swap(own)], axis=0)
    across = ctx_swap(own)
    far = jnp.concatenate([across, core_swap(across)], axis=0)
    return near, far


def reduce_rows(near, far):
    rows = near.shape[0] // 2
    send_far = core_swap(far[rows:].astype(BF16))
    across = ctx_swap((far[:rows] + send_far.astype(F32)).astype(BF16))
    send_near = core_swap(near[rows:].astype(BF16))
    return near[:rows] + send_near.astype(F32) + across.astype(F32)


def lane_masks(width):
    lane = lax.broadcasted_iota(jnp.int32, (1, width), 1)
    return [(lane // DH) == head for head in range(width // DH)]


def attend_kernel(counts, qa, ka, va, qb, kb, vb, oa, ob, probs):
    half = qa.shape[0]
    seq = pl.program_id(0)
    keys = jnp.concatenate([ka[...], kb[...]], axis=0)
    values = jnp.concatenate([va[...], vb[...]], axis=0)
    slot = lax.broadcasted_iota(jnp.int32, (1, 2 * half), 1)
    valid = slot < jnp.where(slot < half, counts[seq, 0], counts[seq, 1] + half)
    masks = lane_masks(keys.shape[1])
    for part, (q_ref, o_ref) in enumerate(((qa, oa), (qb, ob))):
        queries = q_ref[...]
        mixed = None
        for head, mask in enumerate(masks):
            scores = dot_nt(jnp.where(mask, queries, jnp.zeros_like(queries)), keys) * DH ** (-0.5)
            scores = jnp.where(valid, scores, MASKED)
            top = jnp.max(scores, axis=-1, keepdims=True)
            raised = jnp.exp(scores - top)
            low = (raised * (1.0 / jnp.sum(raised, axis=-1, keepdims=True))).astype(BF16)
            probs[0, head, part] = low
            out = dot_nn(low, values)
            mixed = out if mixed is None else jnp.where(mask, out, mixed)
        o_ref[...] = mixed.astype(BF16)


def attend(counts, near, far, seqs, width):
    half = near.shape[0] // seqs
    heads = width // DH
    pairs = heads // 2
    spec = lambda part: pl.BlockSpec(
        (half, 2 * DH), lambda s, p, c, part=part: (s, part * pairs + p)
    )
    out_spec = pl.BlockSpec((half, 2 * DH), lambda s, p, c: (s, p))
    return pl.pallas_call(
        attend_kernel,
        grid_spec=pltpu.PrefetchScalarGridSpec(
            num_scalar_prefetch=1,
            grid=(seqs, pairs),
            in_specs=[spec(0), spec(1), spec(2)] * 2,
            out_specs=[
                out_spec,
                out_spec,
                pl.BlockSpec((1, 2, 2, half, 2 * half), lambda s, p, c: (s, p, 0, 0, 0)),
            ],
        ),
        out_shape=[
            jax.ShapeDtypeStruct((seqs * half, width), BF16),
            jax.ShapeDtypeStruct((seqs * half, width), BF16),
            jax.ShapeDtypeStruct((seqs, heads, 2, half, 2 * half), BF16),
        ],
        cost_estimate=pl.CostEstimate(
            flops=16 * seqs * pairs * half * half * 128, bytes_accessed=8 << 20, transcendentals=4 * half * half * heads
        ),
    )(counts, near, near, near, far, far, far)


def attend_back_kernel(qa, ka, va, ga, qb, kb, vb, gb, probs, dqa, dka, dva, dqb, dkb, dvb):
    half = qa.shape[0]
    keys = jnp.concatenate([ka[...], kb[...]], axis=0)
    values = jnp.concatenate([va[...], vb[...]], axis=0)
    masks = lane_masks(keys.shape[1])
    grad_k = grad_v = None
    for part, (q_ref, g_ref, dq_ref) in enumerate(((qa, ga, dqa), (qb, gb, dqb))):
        queries = q_ref[...]
        grads = g_ref[...]
        dq = dk = dv = None
        for head, mask in enumerate(masks):
            low = probs[0, head, part]
            grad_p = dot_nt(jnp.where(mask, grads, jnp.zeros_like(grads)), values)
            weighted = low.astype(F32) * grad_p
            total = jnp.sum(weighted, axis=-1, keepdims=True)
            grad_s = (weighted - low.astype(F32) * total).astype(BF16)
            dq_h = dot_nn(grad_s, keys)
            dk_h = dot_tn(grad_s, queries)
            dv_h = dot_tn(low, grads)
            dq = dq_h if dq is None else jnp.where(mask, dq_h, dq)
            dk = dk_h if dk is None else jnp.where(mask, dk_h, dk)
            dv = dv_h if dv is None else jnp.where(mask, dv_h, dv)
        dq_ref[...] = (dq * DH ** (-0.5)).astype(BF16)
        grad_k = dk if grad_k is None else grad_k + dk
        grad_v = dv if grad_v is None else grad_v + dv
    grad_k = (grad_k * DH ** (-0.5)).astype(BF16)
    grad_v = grad_v.astype(BF16)
    dka[...] = grad_k[:half]
    dkb[...] = grad_k[half:]
    dva[...] = grad_v[:half]
    dvb[...] = grad_v[half:]


def attend_back(near, far, grad_near, grad_far, probs, seqs, width):
    half = near.shape[0] // seqs
    heads = width // DH
    pairs = heads // 2
    spec = lambda part: pl.BlockSpec((half, 2 * DH), lambda s, p, part=part: (s, part * pairs + p))
    plain = pl.BlockSpec((half, 2 * DH), lambda s, p: (s, p))
    side = jax.ShapeDtypeStruct((seqs * half, width), BF16)
    return pl.pallas_call(
        attend_back_kernel,
        grid=(seqs, pairs),
        in_specs=[spec(0), spec(1), spec(2), plain] * 2
        + [pl.BlockSpec((1, 2, 2, half, 2 * half), lambda s, p: (s, p, 0, 0, 0))],
        out_specs=[plain] * 6,
        out_shape=[side] * 6,
        cost_estimate=pl.CostEstimate(
            flops=40 * seqs * pairs * half * half * 128, bytes_accessed=8 << 20, transcendentals=0
        ),
    )(near, near, near, grad_near, far, far, far, grad_far, probs)


def gather_pack(pack, core):
    mine = lax.dynamic_index_in_dim(pack, core, 0, keepdims=False)
    theirs = core_swap(lax.dynamic_index_in_dim(pack, 1 - core, 0, keepdims=False))
    first = jnp.where(core == 0, mine, theirs)
    second = jnp.where(core == 0, theirs, mine)
    rows, held = mine.shape
    both = jnp.stack([first, second])
    full = lax.all_gather(both, ("fx", "tp"), axis=0, tiled=False)
    groups = full.shape[0]
    tp = lax.axis_size("tp")
    full = full.reshape(groups // tp, tp, 2, rows, held)
    return full.transpose(1, 3, 0, 2, 4).reshape(tp, rows, (groups // tp) * 2 * held)


def scatter_pack(grads, core, ctx):
    tp, rows, width = grads.shape
    fx = lax.axis_size("fx")
    held = width // (2 * fx)
    split = grads.astype(BF16).reshape(tp, rows, fx, 2 * held).transpose(2, 0, 1, 3)
    mine = lax.psum_scatter(
        split.reshape(fx * tp, rows, 2 * held), ("fx", "tp"), scatter_dimension=0, tiled=False
    )
    sides = mine.reshape(rows, 2, held)
    keep = lax.dynamic_index_in_dim(sides, core, 1, keepdims=False)
    recv = core_swap(lax.dynamic_index_in_dim(sides, 1 - core, 1, keepdims=False))
    pair = jnp.stack([jnp.where(core == 0, keep, recv), jnp.where(core == 0, recv, keep)])
    other = ctx_swap(pair)
    return jnp.concatenate([jnp.where(ctx == 0, pair, other), jnp.where(ctx == 0, other, pair)])


def norm_parts(rows):
    mean = jnp.mean(rows, axis=-1, keepdims=True)
    centered = rows - mean
    scale = lax.rsqrt(jnp.mean(centered * centered, axis=-1, keepdims=True) + EPSILON)
    return centered * scale, scale


def norm_back(hat, scale, gain, grads):
    scaled = grads * gain
    grad_rows = scale * (
        scaled
        - jnp.mean(scaled, axis=-1, keepdims=True)
        - hat * jnp.mean(scaled * hat, axis=-1, keepdims=True)
    )
    return grad_rows, jnp.sum(grads * hat, axis=0), jnp.sum(grads, axis=0)


def gelu_parts(inner):
    cumulative = 0.5 * (1.0 + lax.erf(inner * (0.5**0.5)))
    density = jnp.exp(-0.5 * inner * inner) * 0.3989422804014327
    return (inner * cumulative).astype(BF16), (cumulative + inner * density).astype(BF16)


def on_device(
    layer_in, lengths, cotangent, w_query, w_key, w_value, b_query, b_value, w_out, b_out,
    gain_attn, shift_attn, w_up, b_up, w_down, b_down, gain_ffn, shift_ffn,
):
    core, ctx, tp_at = lax.axis_index("core"), lax.axis_index("ctx"), lax.axis_index("tp")
    fs_at = lax.axis_index("fx") * 2 + core
    tp = lax.axis_size("tp")
    fsdp = lax.axis_size("fx") * 2
    seq_count, local_slots, model = layer_in.shape
    held = w_query.shape[0]
    seqs = seq_count // tp
    half = local_slots * tp
    rows = seqs * half
    heads_here = w_query.shape[1] // 4
    units_here = w_up.shape[1] // 4

    def by_sequence(array):
        return lax.all_to_all(array, "tp", 0, 1, tiled=True).reshape(rows, model)

    def by_slot(array):
        return lax.all_to_all(array.reshape(seqs, half, model), "tp", 1, 0, tiled=True)

    own_in = by_sequence(layer_in)
    flat = jnp.concatenate(
        [b_query, b_value, b_up, b_out, gain_attn, shift_attn, b_down, gain_ffn, shift_ffn]
    )
    vectors = lax.all_gather(flat, ("tp", "fx", "core"), axis=0, tiled=False).reshape(tp, fsdp, -1)
    sizes = [b_query.shape[0], b_value.shape[0], b_up.shape[0]]

    def part_vector(start, size):
        whole = vectors[:, :, start : start + size].reshape(tp, 4, fsdp * size // 4)
        return lax.dynamic_index_in_dim(whole, 2 * ctx + core, 1, keepdims=False).reshape(-1).astype(F32)

    def model_vector(index):
        start = sum(sizes) + index * held
        return vectors[0, :, start : start + held].reshape(model).astype(F32)

    bias_q = part_vector(0, sizes[0])
    bias_v = part_vector(sizes[0], sizes[1])
    bias_up = part_vector(sizes[0] + sizes[1], sizes[2])
    bias_out, gain_one, shift_one, bias_down, gain_two, shift_two = (model_vector(i) for i in range(6))
    bias_qkv = jnp.concatenate([bias_q, jnp.zeros_like(bias_q), bias_v])

    def columns(weight, width):
        part = lax.dynamic_slice_in_dim(weight, 2 * ctx * width, 2 * width, 1)
        return part.T.reshape(2, width, held)

    def lines(weight, width):
        return lax.dynamic_slice_in_dim(weight, 2 * ctx * width, 2 * width, 0).reshape(2, width, held)

    pack_qkv = jnp.concatenate([columns(w, heads_here) for w in (w_query, w_key, w_value)], axis=1)
    full_qkv = gather_pack(pack_qkv, core)
    full_qkv = full_qkv.reshape(tp, 3, heads_here, model).transpose(1, 0, 2, 3).reshape(-1, model)
    full_out = gather_pack(lines(w_out, heads_here), core).reshape(-1, model)
    full_up = gather_pack(columns(w_up, units_here), core).reshape(-1, model)
    full_down = gather_pack(lines(w_down, units_here), core).reshape(-1, model)
    width = tp * heads_here

    own_len = lax.dynamic_slice_in_dim(lengths, tp_at * seqs, seqs)
    all_len = jnp.concatenate([own_len, core_swap(own_len)])
    counts = jnp.stack(
        [
            jnp.clip(all_len - ctx * half, 0, half),
            jnp.clip(all_len - (1 - ctx) * half, 0, half),
        ],
        axis=1,
    )

    near_in, far_in = gather_rows(own_in)
    near_qkv = (dot_nt(near_in, full_qkv) + bias_qkv).astype(BF16)
    far_qkv = (dot_nt(far_in, full_qkv) + bias_qkv).astype(BF16)
    near_attn, far_attn, probs = attend(counts, near_qkv, far_qkv, 2 * seqs, width)
    projected = reduce_rows(dot_nn(near_attn, full_out), dot_nn(far_attn, full_out)) + bias_out
    hat_one, scale_one = norm_parts(own_in.astype(F32) + projected)
    normed_one = hat_one * gain_one + shift_one
    near_normed, far_normed = gather_rows(normed_one.astype(BF16))
    near_hidden, near_slope = gelu_parts(dot_nt(near_normed, full_up) + bias_up)
    far_hidden, far_slope = gelu_parts(dot_nt(far_normed, full_up) + bias_up)
    ffn = reduce_rows(dot_nn(near_hidden, full_down), dot_nn(far_hidden, full_down)) + bias_down
    hat_two, scale_two = norm_parts(normed_one + ffn)
    layer_out = by_slot((hat_two * gain_two + shift_two).astype(BF16))

    own_cot = by_sequence(cotangent)
    row_slot = ctx * half + lax.broadcasted_iota(jnp.int32, (seqs, half), 1)
    row_valid = (row_slot < own_len[:, None]).reshape(rows, 1)
    grad_out = jnp.where(row_valid, own_cot.astype(F32), 0.0)
    grad_two, grad_gain_two, grad_shift_two = norm_back(hat_two, scale_two, gain_two, grad_out)
    grad_ffn = grad_two.astype(BF16)
    grad_b_down = jnp.sum(grad_ffn.astype(F32), axis=0)
    near_gffn, far_gffn = gather_rows(grad_ffn)
    near_gpre = (dot_nt(near_gffn, full_down) * near_slope.astype(F32)).astype(BF16)
    far_gpre = (dot_nt(far_gffn, full_down) * far_slope.astype(F32)).astype(BF16)
    grad_down = dot_tn(near_hidden, near_gffn) + dot_tn(far_hidden, far_gffn)
    grad_up = dot_tn(near_gpre, near_normed) + dot_tn(far_gpre, far_normed)
    grad_b_up = jnp.sum(near_gpre.astype(F32), axis=0) + jnp.sum(far_gpre.astype(F32), axis=0)
    grad_normed = reduce_rows(dot_nn(near_gpre, full_up), dot_nn(far_gpre, full_up)) + grad_two
    down_parts = scatter_pack(grad_down.reshape(tp, units_here, model), core, ctx)
    up_parts = scatter_pack(grad_up.reshape(tp, units_here, model), core, ctx)

    grad_one, grad_gain_one, grad_shift_one = norm_back(hat_one, scale_one, gain_one, grad_normed)
    grad_proj = grad_one.astype(BF16)
    grad_b_out = jnp.sum(grad_proj.astype(F32), axis=0)
    near_gproj, far_gproj = gather_rows(grad_proj)
    near_gattn = dot_nt(near_gproj, full_out).astype(BF16)
    far_gattn = dot_nt(far_gproj, full_out).astype(BF16)
    grad_out_w = dot_tn(near_attn, near_gproj) + dot_tn(far_attn, far_gproj)
    dqa, dka, dva, dqb, dkb, dvb = attend_back(
        near_qkv, far_qkv, near_gattn, far_gattn, probs, 2 * seqs, width
    )
    near_dqkv = jnp.concatenate([dqa, dka, dva], axis=1)
    far_dqkv = jnp.concatenate([dqb, dkb, dvb], axis=1)
    input_rows = reduce_rows(dot_nn(near_dqkv, full_qkv), dot_nn(far_dqkv, full_qkv)) + grad_one
    input_grad = by_slot(input_rows.astype(BF16))
    grad_qkv = dot_tn(near_dqkv, near_in) + dot_tn(far_dqkv, far_in)
    grad_b_q = jnp.sum(dqa.astype(F32), axis=0) + jnp.sum(dqb.astype(F32), axis=0)
    grad_b_v = jnp.sum(dva.astype(F32), axis=0) + jnp.sum(dvb.astype(F32), axis=0)

    model_rows = jnp.stack(
        [grad_b_out, grad_gain_one, grad_shift_one, grad_b_down, grad_gain_two, grad_shift_two]
    )
    part_rows = jnp.concatenate(
        [grad_b_up.reshape(tp, -1), grad_b_q.reshape(tp, -1), grad_b_v.reshape(tp, -1)], axis=1
    )
    spare = -part_rows.shape[1] % held
    part_rows = jnp.pad(part_rows, ((0, 0), (0, spare))).reshape(tp, -1, held)
    part_count = part_rows.shape[1]
    vector_rows = jnp.concatenate(
        [
            jnp.broadcast_to(model_rows[None], (tp, 6, model)),
            jnp.tile(part_rows, (1, 1, fsdp)),
        ],
        axis=1,
    )
    pad = -vector_rows.shape[1] % 16
    vector_rows = jnp.pad(vector_rows, ((0, 0), (0, pad), (0, 0)))
    attn_grads = jnp.concatenate(
        [
            grad_qkv.astype(BF16).reshape(3, tp, heads_here, model).transpose(1, 0, 2, 3).reshape(tp, -1, model),
            grad_out_w.astype(BF16).reshape(tp, heads_here, model),
            vector_rows.astype(BF16),
        ],
        axis=1,
    )
    attn_parts = scatter_pack(attn_grads, core, ctx).astype(F32)

    def weight_t(block):
        return attn_parts[:, block * heads_here : (block + 1) * heads_here].reshape(-1, held)

    base = 4 * heads_here
    vector_sums = jnp.sum(attn_parts[:, base : base + 6], axis=0)
    part_all = attn_parts[:, base + 6 : base + 6 + part_count].reshape(4, -1)

    def part_grad(start, size, count):
        whole = part_all[:, start : start + size].reshape(-1)
        return lax.dynamic_slice_in_dim(whole, fs_at * count, count)

    grads = (
        weight_t(0).T,
        weight_t(1).T,
        weight_t(2).T,
        part_grad(units_here, heads_here, sizes[0]),
        part_grad(units_here + heads_here, heads_here, sizes[1]),
        weight_t(3),
        vector_sums[0],
        vector_sums[1],
        vector_sums[2],
        up_parts.astype(F32).reshape(-1, held).T,
        part_grad(0, units_here, sizes[2]),
        down_parts.astype(F32).reshape(-1, held),
        vector_sums[3],
        vector_sums[4],
        vector_sums[5],
    )
    return (layer_out, input_grad) + grads


def solution(mesh):
    fsdp, ctx, tp = (mesh.shape[axis] for axis in ("fsdp", "ctx", "tp"))
    split = Mesh(mesh.devices.reshape(fsdp // 2, 2, ctx, tp), ("fx", "core", "ctx", "tp"))
    fs = ("fx", "core")
    rows = P(fs, ("ctx", "tp"), None)
    wide, tall = P(fs, "tp"), P("tp", fs)
    part, model = P(("tp", "fx", "core")), P(fs)
    weights = (wide, wide, wide, part, part, tall, model, model, model, wide, part, tall, model, model, model)
    return jax.shard_map(
        on_device,
        mesh=split,
        in_specs=(rows, P(fs), rows) + weights,
        out_specs=(rows, rows) + weights,
        check_vma=False,
    )
```

time: 915 us -> 499 us (0.55)
  waiting for transfers between devices: 485 us -> 188 us
  blocking collectives: 172 us -> 64.2 us
  matrix products: 124 us -> 50.8 us
  starting transfers between devices: 1.79 us -> 40.6 us
  Pallas kernels: 0 us -> 21.6 us
  local copies, waits for them, and re-layouts: 57.8 us -> 73.6 us
  other arithmetic: 47 us -> 37.7 us
    reduce_scatter x14 -> x3, waiting for transfers between devices: 285 us -> 74.9 us  [scatter_pack(): lax.psum_scatter(split.reshape(fx * tp, rows, 2 * held), ('fx', 'tp'), sc...]
    all_gather x14 -> x3, waiting for transfers between devices: 196 us -> 0.02 us  [gather_pack(): full = lax.all_gather(both, ('fx', 'tp'), axis=0, tiled=False)]
    ppermute x0 -> x35, waiting for transfers between devices: none -> 84.5 us  [the longest x11 80 us: ctx_swap(): return lax.ppermute(array, 'ctx', SWAP)]
    dot_general x55 -> x24, matrix products: 120 us -> 50.8 us  [the longest x8 22.3 us: dot_nt(): lax.dot_general(left, right, (((1,), (1,)), ((), ())), preferred_element_...]
    all_gather x21 -> x2, blocking collectives: 124 us -> 64.2 us  [the longest x1 34 us: gather_pack(): full = lax.all_gather(both, ('fx', 'tp'), axis=0, tiled=False)]
    psum x2 -> x0, blocking collectives: 29.4 us -> none  [the longest x1 24.1 us: backward_pass(): lax.psum((shards[6], shards[7], shards[8], shards[12], shards[13], shards...]
    all_to_all x0 -> x4, waiting for transfers between devices: none -> 28.8 us  [the longest x2 22.1 us: by_slot(): lax.all_to_all(array.reshape(seqs, half, model), 'tp', 1, 0, tiled=True)]
    dynamic_slice x52 -> x15, local copies, waits for them, and re-layouts: 28.9 us -> 5.23 us  [the longest x3 1.8 us: part_grad(): return lax.dynamic_slice_in_dim(whole, fs_at * count, count)]
  transfers between devices with their start and end apart: 29 -> 45, of which waited for: 19 -> 21; matrix products, arithmetic and copies ran while one was open for 19% -> 25% of each run, Pallas kernels for 0% -> 4%
where the time goes in v1:
time: 499 us; the launch traced here: 493 us
  waiting for transfers between devices  188 us (38%)
  local copies, waits for them, and re-layouts  73.6 us (15%)
  blocking collectives  64.2 us (13%)
  matrix products  50.8 us (10%)
  starting transfers between devices  40.6 us (8%)
  other arithmetic  37.7 us (8%)
  Pallas kernels  21.6 us (4%)
  between operations  16 us (3%)
    ppermute x11, waiting for transfers between devices, ctx_swap(): return lax.ppermute(array, 'ctx', SWAP)  80 us
    reduce_scatter x3, waiting for transfers between devices, scatter_pack(): lax.psum_scatter(split.reshape(fx * tp, rows, 2 * held), ('fx', 'tp'), sc...  74.9 us
    all_gather x1, blocking collectives, gather_pack(): full = lax.all_gather(both, ('fx', 'tp'), axis=0, tiled=False)  34 us
    all_gather x1, blocking collectives, on_device(): lax.all_gather(flat, ('tp', 'fx', 'core'), axis=0, tiled=False)  30.2 us
    dot_general x8, matrix products, dot_nt(): lax.dot_general(left, right, (((1,), (1,)), ((), ())), preferred_element_...  22.3 us
    all_to_all x2, waiting for transfers between devices, by_slot(): lax.all_to_all(array.reshape(seqs, half, model), 'tp', 1, 0, tiled=True)  22.1 us
    unnamed x156, local copies, waits for them, and re-layouts  18.8 us
    ppermute x11, starting transfers between devices, ctx_swap(): return lax.ppermute(array, 'ctx', SWAP)  16.3 us
  transfers between devices with their start and end apart: 45, of which 21 were waited for; matrix products, arithmetic and copies ran while one was open for 25% of the time, Pallas kernels for 4%

profile of v1, /device:TPU:0, one launch (start us, length us, event | category | flops | bytes accessed | tf_op | source)
XLA Modules:
  0.0 492.8 jit_solution(6334603047832596109)
XLA Ops:
  15.2 6.0 %all-to-all-start = ((bf16[4,64,1024]{2,1,0:T(8,128)(2,1)}), bf16[4,64,1024]{2,1,0:T(8,128)(2,1)}, u32[]{:S(2)}, u32[]{:S(2)}) async-start(bf16[4,64,1024]{2,1,0:T(8,128)(2,1)} %param.18), calls=%async_computation | async-start | bytes 1048576 | tf_op jit(solution)/shard_map/all_to_all | solution.py:235
  22.1 30.2 %all-gather.5 = bf16[16,1,1920]{2,1,0:T(2,128)(2,1)S(1)} all-gather(bf16[1,1,1920]{2,1,0:T(2,128)(2,1)S(1)} %reshape.432), channel_id=3, replica_groups=mesh['fx'=2,'core'=2,'ctx'=2,'tp'=4] {'tp','fx','core'}, dimensions={0}, use_global_device_ids=true | all-gather | bytes 65280 | tf_op jit(solution)/shard_map/all_gather | solution.py:244
  53.0 1.6 collective-permute-start.3
  56.6 10.9 %collective-permute-done.3 = bf16[256,1024]{1,0:T(8,128)(2,1)S(1)} collective-permute-done((bf16[256,1024]{1,0:T(8,128)(2,1)}, bf16[256,1024]{1,0:T(8,128)(2,1)S(1)}, u32[]{:S(2)}, u32[]{:S(2)}) %collective-permute-start.3) | collective-permute-done | bytes 524320 | tf_op jit(solution)/shard_map/ppermute | solution.py:23
  67.5 34.0 %all-gather.2 = bf16[16,64,256]{2,1,0:T(8,128)(2,1)S(1)} all-gather(bf16[2,64,256]{2,1,0:T(8,128)(2,1)S(1)} %pad_maximum_fusion.21), channel_id=4, replica_groups=mesh['fx'=2,'core'=2,'ctx'=2,'tp'=4] {'fx','tp'}, dimensions={0}, use_global_device_ids=true | all-gather | bytes 589824 | tf_op jit(solution)/shard_map/all_gather | solution.py:172
  105.7 3.0 copy.159
  110.2 3.7 add_convert_fusion.3.qb.kb.vb
  113.9 3.1 add_convert_fusion.4.qa.ka.va
  117.1 10.5 %shard_map.305 = (bf16[512,256]{1,0:T(8,128)(2,1)}, bf16[512,256]{1,0:T(8,128)(2,1)}, bf16[2,4,2,256,512]{4,3,2,1,0:T(8,128)(2,1)}) custom-call(s32[2,2]{1,0:T(2,128)} %pad_add_fusion.1.counts, bf16[512,768]{1,0:T(8,128)(2,1)} %add_convert_fusion.4.qa.ka.va, bf16[512,768]{1,0:T(8,128)(2,1)} %add_convert_fusion.4.qa.ka.va, ...), custom_call_target="tpu_custom_call" | custom-call | flops 536870912 | bytes 8388608 | tf_op jit(solution)/shard_map/pallas_call | solution.py:89
  127.6 1.5 fusion.79
  131.4 1.8 collective-permute-start.8
  133.2 12.4 %collective-permute-done.8 = bf16[256,1024]{1,0:T(8,128)(2,1)S(1)} collective-permute-done((bf16[256,1024]{1,0:T(8,128)(2,1)S(1)}, bf16[256,1024]{1,0:T(8,128)(2,1)S(1)}, u32[]{:S(2)}, u32[]{:S(2)}) %collective-permute-start.8) | collective-permute-done | bytes 524320 | tf_op jit(solution)/shard_map/ppermute | solution.py:23
  145.7 1.5 fusion.72
  148.5 1.8 collective-permute-start.13
  150.3 11.6 %collective-permute-done.13 = bf16[256,1024]{1,0:T(8,128)(2,1)} collective-permute-done((bf16[256,1024]{1,0:T(8,128)(2,1)S(1)}, bf16[256,1024]{1,0:T(8,128)(2,1)}, u32[]{:S(2)}, u32[]{:S(2)}) %collective-permute-start.13) | collective-permute-done | bytes 524320 | tf_op jit(solution)/shard_map/ppermute | solution.py:23
  161.9 3.8 copy.117
  165.7 2.8 reshape_reshape.14
  168.5 3.7 copy.118
  172.2 2.9 reshape_reshape.15
  177.9 3.3 fusion.81
  181.3 3.5 multiply_convert_fusion.3
  188.2 4.5 all-to-all-start.2
  192.8 3.0 fusion.80
  196.1 2.4 fusion.18
  201.2 6.7 %all-to-all-done.2 = bf16[4,64,1024]{2,1,0:T(8,128)(2,1)S(1)} async-done(((bf16[4,64,1024]{2,1,0:T(8,128)(2,1)}), bf16[4,64,1024]{2,1,0:T(8,128)(2,1)S(1)}, u32[]{:S(2)}, u32[]{:S(2)}) %all-to-all-start.2) | async-done | bytes 524320 | tf_op jit(solution)/shard_map/all_to_all | solution.py:235
  208.3 4.4 collective-permute-done.16
  213.5 1.9 fusion.70
  216.6 1.4 collective-permute-start.19
  218.0 11.8 %collective-permute-done.19 = bf16[256,1024]{1,0:T(8,128)(2,1)S(1)} collective-permute-done((bf16[256,1024]{1,0:T(8,128)(2,1)S(1)}, bf16[256,1024]{1,0:T(8,128)(2,1)S(1)}, u32[]{:S(2)}, u32[]{:S(2)}) %collective-permute-start.19) | collective-permute-done | bytes 524320 | tf_op jit(solution)/shard_map/ppermute | solution.py:23
  229.9 3.1 convert_reduce_fusion.1
  235.1 2.1 convert_reduce_fusion
  238.2 2.8 add_convert_fusion.1
  240.9 4.5 convert_element_type.334
  245.4 3.3 copy.123
  248.8 3.3 fusion.84
  254.5 1.4 collective-permute-start.22
  256.1 12.6 %collective-permute-done.22 = bf16[256,1024]{1,0:T(8,128)(2,1)S(1)} collective-permute-done((bf16[256,1024]{1,0:T(8,128)(2,1)S(1)}, bf16[256,1024]{1,0:T(8,128)(2,1)S(1)}, u32[]{:S(2)}, u32[]{:S(2)}) %collective-permute-start.22) | collective-permute-done | bytes 524320 | tf_op jit(solution)/shard_map/ppermute | solution.py:23
  268.7 2.0 multiply_reduce_fusion.1
  274.9 2.8 add_convert_fusion
  277.7 3.5 convert_element_type.337
  281.2 1.7 copy.128
  283.1 2.6 collective-permute-done.24
  286.8 2.2 convolution_convert_fusion.1.ga
  289.0 1.8 fusion.29
  292.0 11.1 %shard_map.306 = (bf16[512,256]{1,0:T(8,128)(2,1)}, bf16[512,256]{1,0:T(8,128)(2,1)}, bf16[512,256]{1,0:T(8,128)(2,1)}, bf16[512,256]{1,0:T(8,128)(2,1)}, bf16[5...) custom-call(bf16[512,768]{1,0:T(8,128)(2,1)} %add_convert_fusion.4.qa.ka.va, bf16[512,768]{1,0:T(8,128)(2,1)} %add_convert_fusion.4.qa.ka.va, ...), custom_call_target="tpu_custom_call" | custom-call | flops 1342177280 | bytes 8388608 | tf_op jit(solution)/shard_map/pallas_call | solution.py:152
  307.7 1.5 fusion.10
  311.6 2.2 fusion.33
  313.9 2.3 add_convert_fusion.2
  317.5 4.4 maximum_bitcast_fusion
  321.9 1.8 copy.122
  332.2 3.7 reduce.16
  337.1 4.8 all-to-all-start.1
  341.9 2.3 collective-permute-done.28
  344.2 1.7 fusion.35
  346.7 3.7 reduce.17
  351.6 10.2 %all-to-all-done.1 = bf16[4,2,32768]{2,1,0:T(2,128)(2,1)S(1)} async-done(((bf16[4,2,32768]{2,1,0:T(2,128)(2,1)}), bf16[4,2,32768]{2,1,0:T(2,128)(2,1)S(1)}, u32[]{:S(2)}, u32[]{:S(2)}) %all-to-all-start.1) | async-done | bytes 524320 | tf_op jit(solution)/shard_map/all_to_all | solution.py:238
  361.8 3.7 all-to-all-start.3
  368.4 11.9 %all-to-all-done.3 = bf16[4,2,32768]{2,1,0:T(2,128)(2,1)S(1)} async-done(((bf16[4,2,32768]{2,1,0:T(2,128)(2,1)}), bf16[4,2,32768]{2,1,0:T(2,128)(2,1)S(1)}, u32[]{:S(2)}, u32[]{:S(2)}) %all-to-all-start.3) | async-done | bytes 524320 | tf_op jit(solution)/shard_map/all_to_all | solution.py:238
  381.9 14.3 %reduce-scatter.8.cloned.1.call-done = bf16[1,256,512]{2,1,0:T(8,128)(2,1)} async-done(((bf16[8,256,512]{2,1,0:T(8,128)(2,1)}), bf16[1,256,512]{2,1,0:T(8,128)(2,1)}) %reduce-scatter.8.cloned.1.call-update) | async-done | bytes 262160 | tf_op jit(solution)/shard_map/reduce_scatter | solution.py:184
  397.6 1.6 collective-permute-start.32
  400.4 6.5 %collective-permute-done.32 = bf16[2,256,256]{2,1,0:T(8,128)(2,1)S(1)} collective-permute-done((bf16[2,256,256]{2,1,0:T(8,128)(2,1)S(1)}, bf16[2,256,256]{2,1,0:T(8,128)(2,1)S(1)}, u32[]{:S(2)}, u32[]{:S(2)}) %collective-permute-start.32) | collective-permute-done | bytes 262176 | tf_op jit(solution)/shard_map/ppermute | solution.py:23
  407.1 60.6 %reduce-scatter.4.cloned.1.call-done = bf16[1,272,512]{2,1,0:T(8,128)(2,1)} async-done(((bf16[8,272,512]{2,1,0:T(8,128)(2,1)}), bf16[1,272,512]{2,1,0:T(8,128)(2,1)}) %reduce-scatter.4.cloned.1.call-update) | async-done | bytes 278544 | tf_op jit(solution)/shard_map/reduce_scatter | solution.py:184
  470.8 1.6 collective-permute-start.30
  474.8 4.8 collective-permute-done.30
  (365 shorter events, 82.7 us)
Async XLA Ops:
  7.2 98.5 %all-gather.10.cloned.1.call-start = ((), (), s32[]{:S(2)}) async-start(), calls=%async_computation.10 | async-start | bytes 1769472 | tf_op jit(solution)/shard_map/all_gather | solution.py:172
  9.4 4.9 copy-start.58
  9.5 1.5 collective-permute-start.2
  11.0 10.3 %copy-start.48 = (bf16[256,256]{1,0:T(8,128)(2,1)S(1)}, bf16[256,256]{1,0:T(8,128)(2,1)}, u32[]{:S(2)}) copy-start(bf16[256,256]{1,0:T(8,128)(2,1)} %param.26) | copy-start | bytes 393220
  11.7 9.7 %copy-start.47 = (bf16[1024,256]{1,0:T(8,128)(2,1)S(1)}, bf16[1024,256]{1,0:T(8,128)(2,1)}, u32[]{:S(2)}) copy-start(bf16[1024,256]{1,0:T(8,128)(2,1)} %param.32) | copy-start | bytes 1572868
  11.7 150.2 %all-gather.12.cloned.1.call-start = ((), (), s32[]{:S(2)}) async-start(), calls=%async_computation.11 | async-start | bytes 2359296 | tf_op jit(solution)/shard_map/all_gather | solution.py:172
  11.8 10.2 %copy-start.49 = (bf16[64]{0:T(256)(128)(2,1)S(1)}, bf16[64]{0:T(256)(128)(2,1)}, u32[]{:S(2)}) copy-start(bf16[64]{0:T(256)(128)(2,1)} %param.24) | copy-start | bytes 388
  11.8 10.2 %copy-start.50 = (bf16[64]{0:T(256)(128)(2,1)S(1)}, bf16[64]{0:T(256)(128)(2,1)}, u32[]{:S(2)}) copy-start(bf16[64]{0:T(256)(128)(2,1)} %param.25) | copy-start | bytes 388
  11.8 10.2 %copy-start.51 = (bf16[256]{0:T(256)(128)(2,1)S(1)}, bf16[256]{0:T(256)(128)(2,1)}, u32[]{:S(2)}) copy-start(bf16[256]{0:T(256)(128)(2,1)} %param.31) | copy-start | bytes 1540
  11.8 10.1 %copy-start.52 = (bf16[256]{0:T(256)(128)(2,1)S(1)}, bf16[256]{0:T(256)(128)(2,1)}, u32[]{:S(2)}) copy-start(bf16[256]{0:T(256)(128)(2,1)} %param.27) | copy-start | bytes 1540
  11.9 10.1 %copy-start.53 = (bf16[256]{0:T(256)(128)(2,1)S(1)}, bf16[256]{0:T(256)(128)(2,1)}, u32[]{:S(2)}) copy-start(bf16[256]{0:T(256)(128)(2,1)} %param.28) | copy-start | bytes 1540
  11.9 10.1 %copy-start.54 = (bf16[256]{0:T(256)(128)(2,1)S(1)}, bf16[256]{0:T(256)(128)(2,1)}, u32[]{:S(2)}) copy-start(bf16[256]{0:T(256)(128)(2,1)} %param.29) | copy-start | bytes 1540
  11.9 10.1 %copy-start.55 = (bf16[256]{0:T(256)(128)(2,1)S(1)}, bf16[256]{0:T(256)(128)(2,1)}, u32[]{:S(2)}) copy-start(bf16[256]{0:T(256)(128)(2,1)} %param.33) | copy-start | bytes 1540
  11.9 10.1 %copy-start.56 = (bf16[256]{0:T(256)(128)(2,1)S(1)}, bf16[256]{0:T(256)(128)(2,1)}, u32[]{:S(2)}) copy-start(bf16[256]{0:T(256)(128)(2,1)} %param.34) | copy-start | bytes 1540
  11.9 10.1 %copy-start.57 = (bf16[256]{0:T(256)(128)(2,1)S(1)}, bf16[256]{0:T(256)(128)(2,1)}, u32[]{:S(2)}) copy-start(bf16[256]{0:T(256)(128)(2,1)} %param.35) | copy-start | bytes 1540
  12.1 1.4 collective-permute-start.10
  14.9 39.7 %collective-permute-start = (s32[1]{0:T(128)}, s32[1]{0:T(128)}, u32[]{:S(2)}, u32[]{:S(2)}) collective-permute-start(s32[1]{0:T(128)} %dynamic_slice.88), channel_id=1, source_target_pairs={{0,8},{8,0},{1,9},{9,1},{2,10},{10,2},{3,11},{11,3},{4,12},{12,4},... | collective-permute-start | bytes 20 | tf_op jit(solution)/shard_map/ppermute | solution.py:19
  15.2 37.8 %all-to-all-start = ((bf16[4,64,1024]{2,1,0:T(8,128)(2,1)}), bf16[4,64,1024]{2,1,0:T(8,128)(2,1)}, u32[]{:S(2)}, u32[]{:S(2)}) async-start(bf16[4,64,1024]{2,1,0:T(8,128)(2,1)} %param.18), calls=%async_computation | async-start | bytes 1048576 | tf_op jit(solution)/shard_map/all_to_all | solution.py:235
  21.2 147.2 %all-gather.14.cloned.1.call-start = ((), (), s32[]{:S(2)}) async-start(), calls=%async_computation.12 | async-start | bytes 2359296 | tf_op jit(solution)/shard_map/all_gather | solution.py:172
  21.3 35.2 %collective-permute-start.5 = (bf16[64,256]{1,0:T(8,128)(2,1)S(1)}, bf16[64,256]{1,0:T(8,128)(2,1)S(1)}, u32[]{:S(2)}, u32[]{:S(2)}) collective-permute-start(bf16[64,256]{1,0:T(8,128)(2,1)S(1)} %dynamic-slice_bitcast_fusion.4), channel_id=1, source_target_pairs={{0,8},{8,0},{1,9},{9,1},{2,10},{10,2},{3,11},{11,3},{4,12},{12,4},... | collective-permute-start | bytes 98312 | tf_op jit(solution)/shard_map/ppermute | solution.py:19
  21.5 81.7 %collective-permute-start.11 = (bf16[256,256]{1,0:T(8,128)(2,1)S(1)}, bf16[256,256]{1,0:T(8,128)(2,1)S(1)}, u32[]{:S(2)}, u32[]{:S(2)}) collective-permute-start(bf16[256,256]{1,0:T(8,128)(2,1)S(1)} %dynamic-slice_bitcast_fusion.1), channel_id=1, source_target_pairs={{0,8},{8,0},{1,9},{9,1},{2,10},{10,2},{3,11},{11,3},{4,12},{12,4},... | collective-permute-start | bytes 393224 | tf_op jit(solution)/shard_map/ppermute | solution.py:19
  53.0 14.4 %collective-permute-start.3 = (bf16[256,1024]{1,0:T(8,128)(2,1)}, bf16[256,1024]{1,0:T(8,128)(2,1)S(1)}, u32[]{:S(2)}, u32[]{:S(2)}) collective-permute-start(bf16[256,1024]{1,0:T(8,128)(2,1)} %bitcast), channel_id=1, source_target_pairs={{0,4},{4,0},{1,5},{5,1},{2,6},{6,2},{3,7},{7,3},{8,12},{12,8},{9,1... | collective-permute-start | bytes 1572872 | tf_op jit(solution)/shard_map/ppermute | solution.py:23
  67.5 37.4 %collective-permute-start.4 = (bf16[256,1024]{1,0:T(8,128)(2,1)S(1)}, bf16[256,1024]{1,0:T(8,128)(2,1)S(1)}, u32[]{:S(2)}, u32[]{:S(2)}) collective-permute-start(bf16[256,1024]{1,0:T(8,128)(2,1)S(1)} %collective-permute-done.3), channel_id=1, source_target_pairs={{0,8},{8,0},{1,9},{9,1},{2,10},{10,2},{3,11},{11,3},{4,12},{12,4},... | collective-permute-start | bytes 1572872 | tf_op jit(solution)/shard_map/ppermute | solution.py:19
  104.0 10.0 %collective-permute-start.1 = (bf16[256,1024]{1,0:T(8,128)(2,1)}, bf16[256,1024]{1,0:T(8,128)(2,1)}, u32[]{:S(2)}, u32[]{:S(2)}) collective-permute-start(bf16[256,1024]{1,0:T(8,128)(2,1)} %bitcast), channel_id=1, source_target_pairs={{0,8},{8,0},{1,9},{9,1},{2,10},{10,2},{3,11},{11,3},{4,12},{12,4},... | collective-permute-start | bytes 1572872 | tf_op jit(solution)/shard_map/ppermute | solution.py:19
  117.1 10.5 %copy-start.2 = (bf16[256,1024]{1,0:T(8,128)(2,1)S(1)}, bf16[256,1024]{1,0:T(8,128)(2,1)}, u32[]{:S(2)}) copy-start(bf16[256,1024]{1,0:T(8,128)(2,1)} %reshape_reshape.13) | copy-start | bytes 1572868
  129.1 2.1 collective-permute-start.7
  130.2 3.0 collective-permute-start.6
  131.4 14.3 %collective-permute-start.8 = (bf16[256,1024]{1,0:T(8,128)(2,1)S(1)}, bf16[256,1024]{1,0:T(8,128)(2,1)S(1)}, u32[]{:S(2)}, u32[]{:S(2)}) collective-permute-start(bf16[256,1024]{1,0:T(8,128)(2,1)S(1)} %fusion.22), channel_id=1, source_target_pairs={{0,4},{4,0},{1,5},{5,1},{2,6},{6,2},{3,7},{7,3},{8,12},{12,8},{9,1... | collective-permute-start | bytes 1572872 | tf_op jit(solution)/shard_map/ppermute | solution.py:23
  148.5 13.4 %collective-permute-start.13 = (bf16[256,1024]{1,0:T(8,128)(2,1)S(1)}, bf16[256,1024]{1,0:T(8,128)(2,1)}, u32[]{:S(2)}, u32[]{:S(2)}) collective-permute-start(bf16[256,1024]{1,0:T(8,128)(2,1)S(1)} %fusion.28), channel_id=1, source_target_pairs={{0,4},{4,0},{1,5},{5,1},{2,6},{6,2},{3,7},{7,3},{8,12},{12,8},{9,1... | collective-permute-start | bytes 1572872 | tf_op jit(solution)/shard_map/ppermute | solution.py:23
  161.9 14.9 %collective-permute-start.14 = (bf16[256,1024]{1,0:T(8,128)(2,1)}, bf16[256,1024]{1,0:T(8,128)(2,1)}, u32[]{:S(2)}, u32[]{:S(2)}) collective-permute-start(bf16[256,1024]{1,0:T(8,128)(2,1)} %collective-permute-done.13), channel_id=1, source_target_pairs={{0,8},{8,0},{1,9},{9,1},{2,10},{10,2},{3,11},{11,3},{4,12},{12,4},... | collective-permute-start | bytes 1572872 | tf_op jit(solution)/shard_map/ppermute | solution.py:19
  175.1 6.1 %collective-permute-start.9 = (bf16[256,1024]{1,0:T(8,128)(2,1)}, bf16[256,1024]{1,0:T(8,128)(2,1)S(1)}, u32[]{:S(2)}, u32[]{:S(2)}) collective-permute-start(bf16[256,1024]{1,0:T(8,128)(2,1)} %copy-done.16), channel_id=1, source_target_pairs={{0,8},{8,0},{1,9},{9,1},{2,10},{10,2},{3,11},{11,3},{4,12},{12,4},... | collective-permute-start | bytes 1572872 | tf_op jit(solution)/shard_map/ppermute | solution.py:19
  184.7 8.0 %copy-start.19 = (bf16[512,1024]{1,0:T(8,128)(2,1)}, bf16[512,1024]{1,0:T(8,128)(2,1)S(1)}, u32[]{:S(2)}) copy-start(bf16[512,1024]{1,0:T(8,128)(2,1)S(1)} %get-tuple-element.168) | copy-start | bytes 3145732
  188.2 7.9 %collective-permute-start.15 = (bf16[256,1024]{1,0:T(8,128)(2,1)}, bf16[256,1024]{1,0:T(8,128)(2,1)}, u32[]{:S(2)}, u32[]{:S(2)}) collective-permute-start(bf16[256,1024]{1,0:T(8,128)(2,1)} %slice.265), channel_id=1, source_target_pairs={{0,8},{8,0},{1,9},{9,1},{2,10},{10,2},{3,11},{11,3},{4,12},{12,4},... | collective-permute-start | bytes 1572872 | tf_op jit(solution)/shard_map/ppermute | solution.py:19
  188.2 19.7 %all-to-all-start.2 = ((bf16[4,64,1024]{2,1,0:T(8,128)(2,1)}), bf16[4,64,1024]{2,1,0:T(8,128)(2,1)S(1)}, u32[]{:S(2)}, u32[]{:S(2)}) async-start(bf16[4,64,1024]{2,1,0:T(8,128)(2,1)} %param.20), calls=%async_computation.2 | async-start | bytes 1048576 | tf_op jit(solution)/shard_map/all_to_all | solution.py:235
  192.7 172.8 %reduce-scatter.6.cloned.1.call-start = ((), (), s32[]{:S(2)}) async-start(), calls=%async_computation.8 | async-start | bytes 2359296 | tf_op jit(solution)/shard_map/reduce_scatter | solution.py:184
  195.8 12.5 %collective-permute-start.12 = (bf16[256,1024]{1,0:T(8,128)(2,1)S(1)}, bf16[256,1024]{1,0:T(8,128)(2,1)S(1)}, u32[]{:S(2)}, u32[]{:S(2)}) collective-permute-start(bf16[256,1024]{1,0:T(8,128)(2,1)S(1)} %slice.266), channel_id=1, source_target_pairs={{0,8},{8,0},{1,9},{9,1},{2,10},{10,2},{3,11},{11,3},{4,12},{12,4},... | collective-permute-start | bytes 1572872 | tf_op jit(solution)/shard_map/ppermute | solution.py:19
  198.5 14.2 %collective-permute-start.16 = (bf16[256,1024]{1,0:T(8,128)(2,1)}, bf16[256,1024]{1,0:T(8,128)(2,1)S(1)}, u32[]{:S(2)}, u32[]{:S(2)}) collective-permute-start(bf16[256,1024]{1,0:T(8,128)(2,1)} %fusion.18), channel_id=1, source_target_pairs={{0,4},{4,0},{1,5},{5,1},{2,6},{6,2},{3,7},{7,3},{8,12},{12,8},{9,1... | collective-permute-start | bytes 1572872 | tf_op jit(solution)/shard_map/ppermute | solution.py:23
  215.4 14.5 %copy-start.61 = (f32[512,1024]{1,0:T(8,128)S(1)}, f32[512,1024]{1,0:T(8,128)}, u32[]{:S(2)}) copy-start(f32[512,1024]{1,0:T(8,128)} %get-tuple-element.170) | copy-start | bytes 6291460
  215.7 14.2 %copy-start.15 = (bf16[1024,1024]{1,0:T(8,128)(2,1)S(1)}, bf16[1024,1024]{1,0:T(8,128)(2,1)}, u32[]{:S(2)}) copy-start(bf16[1024,1024]{1,0:T(8,128)(2,1)} %reshape_reshape.15) | copy-start | bytes 6291460
  216.6 13.2 %collective-permute-start.19 = (bf16[256,1024]{1,0:T(8,128)(2,1)S(1)}, bf16[256,1024]{1,0:T(8,128)(2,1)S(1)}, u32[]{:S(2)}, u32[]{:S(2)}) collective-permute-start(bf16[256,1024]{1,0:T(8,128)(2,1)S(1)} %get-tuple-element.112), channel_id=1, source_target_pairs={{0,4},{4,0},{1,5},{5,1},{2,6},{6,2},{3,7},{7,3},{8,12},{12,8},{9,1... | collective-permute-start | bytes 1572872 | tf_op jit(solution)/shard_map/ppermute | solution.py:23
  218.0 11.8 %collective-permute-start.17 = (bf16[256,1024]{1,0:T(8,128)(2,1)S(1)}, bf16[256,1024]{1,0:T(8,128)(2,1)S(1)}, u32[]{:S(2)}, u32[]{:S(2)}) collective-permute-start(bf16[256,1024]{1,0:T(8,128)(2,1)S(1)} %get-tuple-element.112), channel_id=1, source_target_pairs={{0,8},{8,0},{1,9},{9,1},{2,10},{10,2},{3,11},{11,3},{4,12},{12,4},... | collective-permute-start | bytes 1572872 | tf_op jit(solution)/shard_map/ppermute | solution.py:19
  229.8 4.6 collective-permute-start.20
  248.8 147.4 %reduce-scatter.8.cloned.1.call-start = ((), (), s32[]{:S(2)}) async-start(), calls=%async_computation.9 | async-start | bytes 2359296 | tf_op jit(solution)/shard_map/reduce_scatter | solution.py:184
  252.2 2.1 collective-permute-start.21
  254.1 2.0 collective-permute-start.18
  254.5 14.3 %collective-permute-start.22 = (bf16[256,1024]{1,0:T(8,128)(2,1)S(1)}, bf16[256,1024]{1,0:T(8,128)(2,1)S(1)}, u32[]{:S(2)}, u32[]{:S(2)}) collective-permute-start(bf16[256,1024]{1,0:T(8,128)(2,1)S(1)} %fusion.15), channel_id=1, source_target_pairs={{0,4},{4,0},{1,5},{5,1},{2,6},{6,2},{3,7},{7,3},{8,12},{12,8},{9,1... | collective-permute-start | bytes 1572872 | tf_op jit(solution)/shard_map/ppermute | solution.py:23
  272.1 14.7 %copy-start.39 = (bf16[256,1024]{1,0:T(8,128)(2,1)}, bf16[256,1024]{1,0:T(8,128)(2,1)S(1)}, u32[]{:S(2)}) copy-start(bf16[256,1024]{1,0:T(8,128)(2,1)S(1)} %get-tuple-element.114) | copy-start | bytes 1572868
  272.1 13.6 %collective-permute-start.24 = (bf16[256,1024]{1,0:T(8,128)(2,1)S(1)}, bf16[256,1024]{1,0:T(8,128)(2,1)}, u32[]{:S(2)}, u32[]{:S(2)}) collective-permute-start(bf16[256,1024]{1,0:T(8,128)(2,1)S(1)} %get-tuple-element.114), channel_id=1, source_target_pairs={{0,4},{4,0},{1,5},{5,1},{2,6},{6,2},{3,7},{7,3},{8,12},{12,8},{9,1... | collective-permute-start | bytes 1572872 | tf_op jit(solution)/shard_map/ppermute | solution.py:23
  274.8 12.0 %collective-permute-start.23 = (bf16[256,1024]{1,0:T(8,128)(2,1)S(1)}, bf16[256,1024]{1,0:T(8,128)(2,1)}, u32[]{:S(2)}, u32[]{:S(2)}) collective-permute-start(bf16[256,1024]{1,0:T(8,128)(2,1)S(1)} %get-tuple-element.114), channel_id=1, source_target_pairs={{0,8},{8,0},{1,9},{9,1},{2,10},{10,2},{3,11},{11,3},{4,12},{12,4},... | collective-permute-start | bytes 1572872 | tf_op jit(solution)/shard_map/ppermute | solution.py:19
  282.9 184.7 %reduce-scatter.4.cloned.1.call-start = ((), (), s32[]{:S(2)}) async-start(), calls=%async_computation.7 | async-start | bytes 2506752 | tf_op jit(solution)/shard_map/reduce_scatter | solution.py:184
  285.7 5.1 %collective-permute-start.25 = (bf16[256,1024]{1,0:T(8,128)(2,1)}, bf16[256,1024]{1,0:T(8,128)(2,1)S(1)}, u32[]{:S(2)}, u32[]{:S(2)}) collective-permute-start(bf16[256,1024]{1,0:T(8,128)(2,1)} %collective-permute-done.24), channel_id=1, source_target_pairs={{0,8},{8,0},{1,9},{9,1},{2,10},{10,2},{3,11},{11,3},{4,12},{12,4},... | collective-permute-start | bytes 1572872 | tf_op jit(solution)/shard_map/ppermute | solution.py:19
  326.2 2.5 collective-permute-start.27
  328.6 13.3 %collective-permute-start.26 = (bf16[256,1024]{1,0:T(8,128)(2,1)}, bf16[256,1024]{1,0:T(8,128)(2,1)S(1)}, u32[]{:S(2)}, u32[]{:S(2)}) collective-permute-start(bf16[256,1024]{1,0:T(8,128)(2,1)} %slice.262), channel_id=1, source_target_pairs={{0,8},{8,0},{1,9},{9,1},{2,10},{10,2},{3,11},{11,3},{4,12},{12,4},... | collective-permute-start | bytes 1572872 | tf_op jit(solution)/shard_map/ppermute | solution.py:19
  329.6 14.6 %collective-permute-start.28 = (bf16[256,1024]{1,0:T(8,128)(2,1)}, bf16[256,1024]{1,0:T(8,128)(2,1)}, u32[]{:S(2)}, u32[]{:S(2)}) collective-permute-start(bf16[256,1024]{1,0:T(8,128)(2,1)} %fusion.11), channel_id=1, source_target_pairs={{0,4},{4,0},{1,5},{5,1},{2,6},{6,2},{3,7},{7,3},{8,12},{12,8},{9,1... | collective-permute-start | bytes 1572872 | tf_op jit(solution)/shard_map/ppermute | solution.py:23
  331.7 12.5 %copy-start.4 = (f32[256,1024]{1,0:T(8,128)S(1)}, f32[256,1024]{1,0:T(8,128)}, u32[]{:S(2)}) copy-start(f32[256,1024]{1,0:T(8,128)} %get-tuple-element.115) | copy-start | bytes 3145732
  337.1 24.7 %all-to-all-start.1 = ((bf16[4,2,32768]{2,1,0:T(2,128)(2,1)}), bf16[4,2,32768]{2,1,0:T(2,128)(2,1)S(1)}, u32[]{:S(2)}, u32[]{:S(2)}) async-start(bf16[4,2,32768]{2,1,0:T(2,128)(2,1)} %reshape.448), calls=%async_computation.1 | async-start | bytes 1048576 | tf_op jit(solution)/shard_map/all_to_all | solution.py:238
  361.8 18.5 %all-to-all-start.3 = ((bf16[4,2,32768]{2,1,0:T(2,128)(2,1)}), bf16[4,2,32768]{2,1,0:T(2,128)(2,1)S(1)}, u32[]{:S(2)}, u32[]{:S(2)}) async-start(bf16[4,2,32768]{2,1,0:T(2,128)(2,1)} %reshape.450), calls=%async_computation.3 | async-start | bytes 1048576 | tf_op jit(solution)/shard_map/all_to_all | solution.py:238
  366.8 30.8 %collective-permute-start.31 = (bf16[256,256]{1,0:T(8,128)(2,1)S(1)}, bf16[256,256]{1,0:T(8,128)(2,1)S(1)}, u32[]{:S(2)}, u32[]{:S(2)}) collective-permute-start(bf16[256,256]{1,0:T(8,128)(2,1)S(1)} %bitcast.304), channel_id=1, source_target_pairs={{0,8},{8,0},{1,9},{9,1},{2,10},{10,2},{3,11},{11,3},{4,12},{12,4},... | collective-permute-start | bytes 393224 | tf_op jit(solution)/shard_map/ppermute | solution.py:19
  397.4 1.8 collective-permute-start.33
  397.6 9.2 %collective-permute-start.32 = (bf16[2,256,256]{2,1,0:T(8,128)(2,1)S(1)}, bf16[2,256,256]{2,1,0:T(8,128)(2,1)S(1)}, u32[]{:S(2)}, u32[]{:S(2)}) collective-permute-start(bf16[2,256,256]{2,1,0:T(8,128)(2,1)S(1)} %pad_maximum_fusion.17), channel_id=1, source_target_pairs={{0,4},{4,0},{1,5},{5,1},{2,6},{6,2},{3,7},{7,3},{8,12},{12,8},{9,1... | collective-permute-start | bytes 786440 | tf_op jit(solution)/shard_map/ppermute | solution.py:23
  399.2 70.1 %collective-permute-start.34 = (bf16[2,256,256]{2,1,0:T(8,128)(2,1)S(1)}, bf16[2,256,256]{2,1,0:T(8,128)(2,1)S(1)}, u32[]{:S(2)}, u32[]{:S(2)}) collective-permute-start(bf16[2,256,256]{2,1,0:T(8,128)(2,1)S(1)} %pad_maximum_fusion.18), channel_id=1, source_target_pairs={{0,4},{4,0},{1,5},{5,1},{2,6},{6,2},{3,7},{7,3},{8,12},{12,8},{9,1... | collective-permute-start | bytes 786440 | tf_op jit(solution)/shard_map/ppermute | solution.py:23
  469.3 1.4 collective-permute-start.29
  470.8 8.8 %collective-permute-start.30 = (bf16[2,272,256]{2,1,0:T(8,128)(2,1)S(1)}, bf16[2,272,256]{2,1,0:T(8,128)(2,1)S(1)}, u32[]{:S(2)}, u32[]{:S(2)}) collective-permute-start(bf16[2,272,256]{2,1,0:T(8,128)(2,1)S(1)} %pad_maximum_fusion.14), channel_id=1, source_target_pairs={{0,4},{4,0},{1,5},{5,1},{2,6},{6,2},{3,7},{7,3},{8,12},{12,8},{9,1... | collective-permute-start | bytes 835592 | tf_op jit(solution)/shard_map/ppermute | solution.py:23
  479.7 6.0 %copy-start.1 = (bf16[256,1024]{1,0:T(8,128)(2,1)S(1)}, bf16[256,1024]{1,0:T(8,128)(2,1)}, u32[]{:S(2)}) copy-start(bf16[256,1024]{1,0:T(8,128)(2,1)} %param.30) | copy-start | bytes 1572868
  (43 other events, 113.0 us)
Sparse Core Ops, SparseCore 0:
  11.8 53.1 all-gather.9
  67.7 49.5 all-gather.11
  120.0 48.4 all-gather.13
  248.9 69.2 reduce-scatter.5
  321.5 74.5 reduce-scatter.7
  399.5 68.1 reduce-scatter.3
